TPU v7x, 32 devices: a whole 2x2x4 slice. The times are simulated.
32 devices in a mesh: section: 1, dp: 32 (over z, y, x, core).
Axes of the slice: x: 2, y: 2, z: 4, core: 2. Of those that a mesh axis runs over, the one named last changes fastest.
Arguments:
- tokens: bfloat16 [4096, 8192], P('dp'), may hold values from -6 to 6
- blocks_in: bfloat16 [1, 160, 128, 128], P('section', 'dp'), may hold values from -0.078125 to 0.078125
- blocks_out: bfloat16 [1, 160, 128, 128], P('section', 'dp'), may hold values from -0.3125 to 0.3125
- pos_in: int32 [1, 160], P('section', 'dp'), may hold values from 0 to 256, as said below
- pos_out: int32 [1, 160], P('section', 'dp'), may hold values from 0 to 256, as said below
- cotangent: bfloat16 [4096, 8192], P('dp'), may hold values from -0.08984375 to 0.08984375
Outputs:
- grad_in: bfloat16 [1, 160, 128, 128], P('section', 'dp')
- grad_out: bfloat16 [1, 160, 128, 128], P('section', 'dp')
Inputs may be any that keep to these rules, and one draw needn't show every extreme that they name: For each layer the first k slots (k from 110 to 160) hold distinct block numbers and the other slots hold 256, marking an empty slot; in each of pos_in and pos_out some layer fills all 160 slots. `pos_out`: as for pos_in, drawn independently.
All inputs are finite; a program needn't handle non-finite values.
Results may differ from a plain program's by a relative error of at most 0.023.
Values may be sent and summed in bfloat16 or wider, within the bound.
A program may use at most 128 MiB of HBM per device.

v0:
```python
import functools

import jax
import jax.numpy as jnp
from jax import lax
from jax.experimental import pallas as pl
from jax.experimental.pallas import tpu as pltpu
from jax.sharding import PartitionSpec as P

D = 8192
RANK = 512
BLOCK = 128
MICRO = 2


EPS = 1e-05


def from_behind(block, axis, distance):
    devices = range(lax.axis_size(axis))
    route = [(i - distance, i) for i in devices if i - distance in devices]
    return lax.ppermute(block, axis, route)


def expand(blocks, places, rows_b, cols_b):
    flat = jnp.zeros((rows_b * cols_b, BLOCK, BLOCK), blocks.dtype)
    flat = flat.at[places].set(blocks, mode="drop")
    return (
        flat.reshape(rows_b, cols_b, BLOCK, BLOCK)
        .transpose(0, 2, 1, 3)
        .reshape(rows_b * BLOCK, cols_b * BLOCK)
    )


def slot_grads(left, right, places, rows_b, cols_b):
    count = left.shape[0]
    valid = places < rows_b * cols_b
    row_block = jnp.where(valid, places // cols_b, 0).astype(jnp.int32)
    col_block = jnp.where(valid, places % cols_b, 0).astype(jnp.int32)
    left_blocks = jnp.take(left.reshape(count, rows_b, BLOCK), row_block, axis=1)
    right_blocks = jnp.take(right.reshape(count, cols_b, BLOCK), col_block, axis=1)
    result = jnp.einsum(
        "tjb,tjc->jbc", left_blocks, right_blocks, preferred_element_type=jnp.float32
    )
    return jnp.where(valid[:, None, None], result, 0.0)


def norm_parts(hidden):
    wide = hidden.astype(jnp.float32)
    scale = jnp.sqrt(jnp.mean(wide * wide, axis=-1, keepdims=True) + EPS)
    return (wide, scale)


def forward_layer(hidden, mat_a, mat_b):
    wide, scale = norm_parts(hidden)
    normed = (wide / scale).astype(jnp.bfloat16)
    pre = jnp.dot(normed, mat_a, preferred_element_type=jnp.float32)
    act = (pre * jax.nn.sigmoid(pre)).astype(jnp.bfloat16)
    return (wide + jnp.dot(act, mat_b, preferred_element_type=jnp.float32)).astype(jnp.bfloat16)


def backward_layer(hidden, upstream, mat_a, mat_b):
    wide, scale = norm_parts(hidden)
    unit = wide / scale
    normed = unit.astype(jnp.bfloat16)
    pre = jnp.dot(normed, mat_a, preferred_element_type=jnp.float32)
    sig = jax.nn.sigmoid(pre)
    act = (pre * sig).astype(jnp.bfloat16)
    dact = lax.dot_general(
        upstream, mat_b, (((1,), (1,)), ((), ())), preferred_element_type=jnp.float32
    )
    dpre = (dact * sig * (1.0 + pre * (1.0 - sig))).astype(jnp.bfloat16)
    dnorm = lax.dot_general(
        dpre, mat_a, (((1,), (1,)), ((), ())), preferred_element_type=jnp.float32
    )
    inner = jnp.mean(dnorm * unit, axis=-1, keepdims=True)
    earlier = (upstream.astype(jnp.float32) + (dnorm - unit * inner) / scale).astype(jnp.bfloat16)
    return (earlier, normed, dpre, act)


def store(stack, value, picked, active):
    updated = lax.dynamic_update_slice_in_dim(stack, value[None], picked, 0)
    return jnp.where(active, updated, stack)


def per_device(tokens, blocks_in, blocks_out, pos_in, pos_out, cotangent):
    sections = lax.axis_size("section")
    here = lax.axis_index("section")
    rows_d = D // BLOCK
    rows_k = RANK // BLOCK
    full_in, full_out, all_in, all_out = (
        lax.all_gather(blocks_in, "dp", axis=1, tiled=True),
        lax.all_gather(blocks_out, "dp", axis=1, tiled=True),
        lax.all_gather(pos_in, "dp", axis=1, tiled=True),
        lax.all_gather(pos_out, "dp", axis=1, tiled=True),
    )
    mat_a = expand(full_in[0], all_in[0], rows_d, rows_k)
    mat_b = expand(full_out[0], all_out[0], rows_k, rows_d)
    micro_rows = tokens.shape[0] // MICRO
    turns = MICRO + sections - 1
    saved = jnp.zeros((MICRO, micro_rows, D), jnp.bfloat16)
    carried = jnp.zeros((micro_rows, D), jnp.bfloat16)
    for turn in range(turns):
        micro = turn - here
        active = (micro >= 0) & (micro < MICRO)
        picked = jnp.clip(micro, 0, MICRO - 1)
        first = lax.dynamic_slice_in_dim(tokens, picked * micro_rows, micro_rows, 0)
        entering = jnp.where(here == 0, first, carried)
        saved = store(saved, entering, picked, active)
        if turn < turns - 1:
            leaving = lax.cond(
                active, lambda x: forward_layer(x, mat_a, mat_b), lambda x: x, entering
            )
            carried = from_behind(leaving, "section", 1)
    kept_normed = jnp.zeros((MICRO, micro_rows, D), jnp.bfloat16)
    kept_dpre = jnp.zeros((MICRO, micro_rows, RANK), jnp.bfloat16)
    kept_act = jnp.zeros((MICRO, micro_rows, RANK), jnp.bfloat16)
    kept_upper = jnp.zeros((MICRO, micro_rows, D), jnp.bfloat16)
    carried_grad = jnp.zeros((micro_rows, D), jnp.bfloat16)
    for turn in range(turns):
        micro = turn - (sections - 1 - here)
        active = (micro >= 0) & (micro < MICRO)
        picked = jnp.clip(micro, 0, MICRO - 1)
        last = lax.dynamic_slice_in_dim(cotangent, picked * micro_rows, micro_rows, 0)
        upstream = jnp.where(here == sections - 1, last, carried_grad)
        hidden = lax.dynamic_index_in_dim(saved, picked, 0, keepdims=False)

        def run_layer():
            return backward_layer(hidden, upstream, mat_a, mat_b)

        def skip_layer():
            return (
                upstream,
                jnp.zeros((micro_rows, D), jnp.bfloat16),
                jnp.zeros((micro_rows, RANK), jnp.bfloat16),
                jnp.zeros((micro_rows, RANK), jnp.bfloat16),
            )

        earlier, normed, dpre, act = lax.cond(active, run_layer, skip_layer)
        kept_normed = store(kept_normed, normed, picked, active)
        kept_dpre = store(kept_dpre, dpre, picked, active)
        kept_act = store(kept_act, act, picked, active)
        kept_upper = store(kept_upper, upstream, picked, active)
        if turn < turns - 1:
            carried_grad = from_behind(earlier, "section", -1)
    all_rows = MICRO * micro_rows
    terms_in = slot_grads(
        kept_normed.reshape(all_rows, D),
        kept_dpre.reshape(all_rows, RANK),
        all_in[0],
        rows_d,
        rows_k,
    )[None]
    terms_out = slot_grads(
        kept_act.reshape(all_rows, RANK),
        kept_upper.reshape(all_rows, D),
        all_out[0],
        rows_k,
        rows_d,
    )[None]
    sums_in, sums_out = (
        lax.psum_scatter(
            terms_in.astype(jnp.bfloat16), "dp", scatter_dimension=1, tiled=True
        ).astype(jnp.float32),
        lax.psum_scatter(
            terms_out.astype(jnp.bfloat16), "dp", scatter_dimension=1, tiled=True
        ).astype(jnp.float32),
    )
    return (sums_in.astype(jnp.bfloat16), sums_out.astype(jnp.bfloat16))


EXTRA= 16
WIDE = 1024


class Place:
    def __init__(self, devices):
        me = lax.axis_index("dp")
        self.depth = devices // 8
        self.me = me
        self.core = me % 2
        self.chip = me // 2
        x = self.chip % 2
        y = (self.chip // 2) % 2
        self.z = self.chip // 4
        dx = 1 - 2 * x
        dy = 2 * (1 - 2 * y)
        self.first = (1 - self.core) * dx + self.core * dy
        self.second = (1 - self.core) * dy + self.core * dx
        self.sibling = me + 1 - 2 * self.core

    def member(self, ds, df, dz, first=None, second=None):
        first = self.first if first is None else first
        second = self.second if second is None else second
        along = ((self.z + dz) % self.depth - self.z) * 4
        return self.chip + along + df * first + ds * second

    def device(self, ds, df, dz):
        return 2 * self.member(ds, df, dz) + self.core

    def knock(self):
        peers = [self.sibling, self.device(1, 0, 0), self.device(0, 1, 0)]
        peers += [self.device(0, 0, d) for d in range(1, self.depth)]
        barrier = pltpu.get_barrier_semaphore()
        for peer in peers:
            pl.semaphore_signal(
                barrier, inc=1, device_id={"dp": peer}, device_id_type=pl.DeviceIdType.MESH
            )
        return lambda: pl.semaphore_wait(barrier, len(peers))


def remote(src, dst, send, recv, peer):
    return pltpu.make_async_remote_copy(
        src_ref=src,
        dst_ref=dst,
        send_sem=send,
        recv_sem=recv,
        device_id={"dp": peer},
        device_id_type=pl.DeviceIdType.MESH,
    )


def gather_kernel(
    devices, own_in, own_out, own_tags, tokens, cotangent, full, tags, other, send_sems, chip_sems, misc_sems
):
    at = Place(devices)
    depth = at.depth
    mine = at.core
    sends = []

    def on_core(core):
        return pl.when(mine == core)

    def local_copy(source):
        return pltpu.make_async_copy(source, full.at[at.me], misc_sems.at[0])

    on_core(0)(lambda: local_copy(own_in).start())
    on_core(1)(lambda: local_copy(own_out).start())
    local = [
        local_copy(own_in),
        pltpu.make_async_copy(own_tags.at[mine], tags.at[at.me], misc_sems.at[3]),
    ]
    local[1].start()
    at.knock()()

    def start(src, dst, recv, peer, like, present=None):
        remote(src, dst, send_sems.at[len(sends)], recv, peer).start()
        sends.append((like, present))

    def pair_copy(source):
        return remote(source, full.at[at.me], send_sems.at[0], misc_sems.at[1], at.sibling)

    on_core(0)(lambda: pair_copy(own_out).start())
    on_core(1)(lambda: pair_copy(own_in).start())
    sends.append((own_in, None))
    start(own_tags.at[1 - mine], tags.at[at.me], misc_sems.at[4], at.sibling, own_tags.at[0])
    pair = [
        pair_copy(own_in),
        remote(own_tags.at[0], tags.at[at.me], send_sems.at[0], misc_sems.at[4], at.sibling),
    ]

    per = own_in.shape[0]
    bulk = full.at[pl.ds(0, 2), pl.ds(0, per - 1)]
    spare = full.at[pl.ds(0, 2), pl.ds(per - 1, 1)]

    def odd(chip):
        return full.at[pl.ds(2 * chip, 2), pl.ds(per - 1, 1)]

    def push_odd(chip, peer, present=None):
        start(odd(chip), odd(chip), chip_sems.at[2, chip], peer, spare, present)

    def odd_arrived(chip):
        remote(odd(chip), odd(chip), send_sems.at[0], chip_sems.at[2, chip], at.sibling).wait_recv()

    def shards(chip):
        return (
            (full.at[pl.ds(2 * chip, 2), pl.ds(0, per - 1)], chip_sems.at[0, chip]),
            (tags.at[pl.ds(2 * chip, 2)], chip_sems.at[1, chip]),
        )

    def push(chip, peer, present=None):
        for (shard, sem), like in zip(shards(chip), (bulk, tags.at[pl.ds(0, 2)])):
            start(shard, shard, sem, peer, like, present)

    def arrived(chip):
        for shard, sem in shards(chip):
            remote(shard, shard, send_sems.at[0], sem, at.sibling).wait_recv()

    first, second = at.device(0, 1, 0), at.device(1, 0, 0)
    above, below = at.me + 8, at.me - 8
    up, down = at.z + 1 < depth, at.z >= 1
    for copy in local:
        copy.wait()
    for copy in pair:
        copy.wait_recv()
    here = at.chip
    pl.when(up)(lambda: push(here, above, lambda: up))
    pl.when(down)(lambda: push(here, below, lambda: down))
    push(here, second)
    push(here, first)
    push_odd(here, first)
    push_odd(here, second)
    pl.when(up)(lambda: push_odd(here, above, lambda: up))
    pl.when(down)(lambda: push_odd(here, below, lambda: down))
    swap = misc_sems.at[2]
    give = remote(tokens, other, send_sems.at[len(sends)], swap, at.sibling)
    keep = remote(cotangent, other, send_sems.at[len(sends)], swap, at.sibling)
    on_core(0)(lambda: keep.start())
    on_core(1)(lambda: give.start())
    sends.append((tokens, None))
    facing = here + at.first
    arrived(facing)
    push(facing, second)
    plane = [here, facing, here + at.second, facing + at.second]
    for q in plane[1:]:
        odd_arrived(q)
        if q is facing:
            push_odd(q, second)
        pl.when(up)(lambda q=q: push_odd(q, above, lambda: up))
        pl.when(down)(lambda q=q: push_odd(q, below, lambda: down))

    def odd_line(d):
        low, high = at.z >= d, at.z + d < depth
        for q in plane:

            def odd_below(q=q):
                odd_arrived(q - 4 * d)
                pl.when(up)(lambda: push_odd(q - 4 * d, above, lambda: low & up))

            def odd_above(q=q):
                odd_arrived(q + 4 * d)
                pl.when(down)(lambda: push_odd(q + 4 * d, below, lambda: high & down))

            pl.when(low)(odd_below)
            pl.when(high)(odd_above)

    for d in range(1, depth):
        low, high = at.z >= d, at.z + d < depth

        def from_below(d=d, low=low):
            arrived(here - 4 * d)
            pl.when(up)(lambda: push(here - 4 * d, above, lambda: low & up))
            push(here - 4 * d, first, lambda: low)
            push(here - 4 * d, second, lambda: low)

        def from_above(d=d, high=high):
            arrived(here + 4 * d)
            pl.when(down)(lambda: push(here + 4 * d, below, lambda: high & down))
            push(here + 4 * d, first, lambda: high)
            push(here + 4 * d, second, lambda: high)

        def relay_below(d=d, low=low):
            arrived(facing - 4 * d)
            push(facing - 4 * d, second, lambda: low)

        def relay_above(d=d, high=high):
            arrived(facing + 4 * d)
            push(facing + 4 * d, second, lambda: high)

        pl.when(low)(from_below)
        pl.when(high)(from_above)
        pl.when(low)(relay_below)
        pl.when(high)(relay_above)
        if d > 1:
            odd_line(d - 1)
    if depth > 1:
        odd_line(depth - 1)
    for df in range(2):
        for d in range(depth):
            arrived(at.member(1, df, d))
    give.wait_recv()
    for n, (like, present) in enumerate(sends):

        def sent(n=n, like=like):
            remote(like, like, send_sems.at[n], misc_sems.at[0], at.sibling).wait_send()

        if present is None:
            sent()
        else:
            pl.when(present())(sent)


def gather_blocks(own_in, own_out, own_tags, tokens, cotangent, devices):
    chips = devices // 2
    depth = devices // 8
    sends = 2 * (1 + 2 + 2 + 1 + 8 * (depth - 1)) + 1 + 11 + 8 * (depth - 1)
    anywhere = pl.BlockSpec(memory_space=pl.ANY)
    return pl.pallas_call(
        functools.partial(gather_kernel, devices),
        out_shape=(
            jax.ShapeDtypeStruct((devices,) + own_in.shape, own_in.dtype),
            jax.ShapeDtypeStruct((devices,) + own_tags.shape[1:], own_tags.dtype),
            jax.ShapeDtypeStruct(tokens.shape, tokens.dtype),
        ),
        in_specs=[pl.BlockSpec(memory_space=pltpu.VMEM)] * 3 + [anywhere, anywhere],
        out_specs=(anywhere, anywhere, anywhere),
        scratch_shapes=[
            pltpu.SemaphoreType.DMA((sends,)),
            pltpu.SemaphoreType.DMA((3, chips)),
            pltpu.SemaphoreType.DMA((5,)),
        ],
        compiler_params=pltpu.CompilerParams(collective_id=0, has_side_effects=True),
        name="gather_blocks",
    )(own_in, own_out, own_tags, tokens, cotangent)


def layer_kernel(devices, per, pos, begin, tokens, cotangent, other, full, out,
                 blocks, rows, mat_a, mat_b, grads, middle, packed, middle_got, inverse,
                 held, second_got, first_got, line_got, last_got,
                 load_sems, send_sems, second_sems, first_sems, line_sems, pair_sems):
    at = Place(devices)
    depth = at.depth
    mine = at.core
    count, width = tokens.shape
    rank = mat_a.shape[1]
    rows_k = rank // BLOCK
    rows_d = width // BLOCK
    chunks = [slice(i, i + WIDE) for i in range(0, width, WIDE)]
    sends = []

    def start(src, dst, recv, peer):
        copy = remote(src, dst, send_sems.at[len(sends)], recv, peer)
        copy.start()
        sends.append(copy)
        return copy

    def got(buf, sem):
        remote(buf, buf, send_sems.at[0], sem, at.sibling).wait_recv()

    used = full.shape[0]
    load_blocks = pltpu.make_async_copy(full, blocks.at[pl.ds(0, used)], load_sems.at[0])
    load_blocks.start()
    load_own = pltpu.make_async_copy(tokens, rows.at[pl.ds(mine * count, count)], load_sems.at[1])

    @pl.when(mine == 0)
    def _():
        load_own.start()

    @pl.when(mine == 1)
    def _():
        pltpu.make_async_copy(cotangent, rows.at[pl.ds(mine * count, count)], load_sems.at[1]).start()

    load_other = pltpu.make_async_copy(other, rows.at[pl.ds((1 - mine) * count, count)], load_sems.at[2])
    load_other.start()
    wait_peers = at.knock()
    blocks[used] = jnp.zeros((BLOCK, BLOCK), jnp.bfloat16)
    grads[rows_d * rows_k] = jnp.zeros((BLOCK, BLOCK), jnp.bfloat16)
    load_blocks.wait()

    def slot_of(b):
        return blocks[begin[b]]

    @pl.when(mine == 0)
    def _():
        def expand_a(r, carry):
            into = pl.ds(pl.multiple_of(r * BLOCK, BLOCK), BLOCK)
            for c in range(rows_k):
                mat_a[into, c * BLOCK : (c + 1) * BLOCK] = slot_of(r * rows_k + c)
            return carry

        lax.fori_loop(0, rows_d, expand_a, 0)

    @pl.when(mine == 1)
    def _():
        def expand_b(c, carry):
            into = pl.ds(pl.multiple_of(c * BLOCK, BLOCK), BLOCK)
            for r in range(rows_k):
                mat_b[r * BLOCK : (r + 1) * BLOCK, into] = slot_of(r * rows_d + c)
            return carry

        lax.fori_loop(0, rows_d, expand_b, 0)

    load_own.wait()
    load_other.wait()

    @pl.when(mine == 0)
    def _():
        total = jnp.zeros((2 * count, BLOCK), jnp.float32)
        for k in range(0, width, BLOCK):
            wide = rows[:, k : k + BLOCK].astype(jnp.float32)
            total += wide * wide
        scale = jnp.sqrt(jnp.sum(total, axis=-1, keepdims=True) / width + EPS)
        inverse[...] = jnp.broadcast_to(1.0 / scale, inverse.shape)
        pre = jnp.zeros((2 * count, rank), jnp.float32)
        for k in chunks:
            pre += jnp.dot(rows[:, k], mat_a[k, :], preferred_element_type=jnp.float32)
        middle[...] = pre * inverse[:, :1]

    @pl.when(mine == 1)
    def _():
        dact = jnp.zeros((2 * count, rank), jnp.float32)
        for k in chunks:
            dact += lax.dot_general(
                rows[:, k], mat_b[:, k], (((1,), (1,)), ((), ())), preferred_element_type=jnp.float32
            )
        middle[...] = dact

    wait_peers()
    packed[...] = middle[...].astype(jnp.bfloat16)
    start(packed, middle_got, pair_sems.at[0], at.sibling).wait_recv()
    across = (((0,), (0,)), ((), ()))

    @pl.when(mine == 0)
    def _():
        pre = middle[...]
        sig = jax.nn.sigmoid(pre)
        dpre = middle_got[...].astype(jnp.float32) * sig * (1.0 + pre * (1.0 - sig))
        dpre = (dpre * inverse[:, :1]).astype(jnp.bfloat16)
        for k in chunks:
            part = lax.dot_general(
                rows[:, k], dpre, across, preferred_element_type=jnp.float32
            ).astype(jnp.bfloat16)
            for r in range(WIDE // BLOCK):
                for c in range(rows_k):
                    grads[(k.start // BLOCK + r) * rows_k + c] = part[
                        r * BLOCK : (r + 1) * BLOCK, c * BLOCK : (c + 1) * BLOCK
                    ]

    @pl.when(mine == 1)
    def _():
        pre = middle_got[...].astype(jnp.float32)
        act = (pre * jax.nn.sigmoid(pre)).astype(jnp.bfloat16)
        for k in chunks:
            part = lax.dot_general(
                act, rows[:, k], across, preferred_element_type=jnp.float32
            ).astype(jnp.bfloat16)
            for r in range(rows_k):
                for c in range(WIDE // BLOCK):
                    grads[r * rows_d + k.start // BLOCK + c] = part[
                        r * BLOCK : (r + 1) * BLOCK, c * BLOCK : (c + 1) * BLOCK
                    ]

    line = sorted(range(1, depth), key=lambda d: (min(d, depth - d), d))
    dist = line[::-1] + [0]
    order = [(ds, df, d) for ds in (1, 0) for d in dist for df in (1, 0)]
    for i, (ds, df, dz) in enumerate(order):
        chip = at.member(ds, df, dz)
        parts = []
        if not ds:
            parts.append(second_got.at[df * depth + dz])
            got(parts[-1], second_sems.at[df * depth + dz])
        if not ds and not df:
            parts.append(first_got.at[dz])
            got(parts[-1], first_sems.at[dz])
            if not dz:
                for d in range(1, depth):
                    parts.append(line_got.at[d - 1])
                    got(parts[-1], line_sems.at[d - 1])

        def fill(step, carry, i=i, parts=parts, chip=chip):
            half = step // per
            part = pl.ds(pl.multiple_of((step % per) * BLOCK, BLOCK), BLOCK)
            value = grads[pos[chip * (2 * per) + step]]
            if parts:
                value = value.astype(jnp.float32)
                for q in parts:
                    value += q[half, part, :].astype(jnp.float32)
            held[i, half, part, :] = value.astype(jnp.bfloat16)
            return carry

        lax.fori_loop(0, 2 * per, fill, 0)
        if ds:
            start(held.at[i], second_got.at[df * depth + dz], second_sems.at[df * depth + dz], at.device(1, 0, 0))
        elif df:
            start(held.at[i], first_got.at[dz], first_sems.at[dz], at.device(0, 1, 0))
        elif dz:
            start(held.at[i], line_got.at[dz - 1], line_sems.at[dz - 1], at.device(0, 0, dz))
        else:
            last = start(held.at[i, 1 - mine], last_got, pair_sems.at[1], at.sibling)
            out[mine] = held[i, mine]
            last.wait_recv()
    out[1 - mine] = last_got[...]
    for copy in sends:
        copy.wait_send()


def layer_sums(places, begin, tokens, cotangent, other, full, devices, per):
    count, width = tokens.shape
    chips = devices // 2
    depth = devices // 8
    shard = (2, per * BLOCK, BLOCK)
    dma = pltpu.SemaphoreType.DMA
    vmem = pltpu.VMEM
    anywhere = pl.BlockSpec(memory_space=pl.ANY)
    scalars = pl.BlockSpec(memory_space=pltpu.SMEM)
    bf16, f32 = jnp.bfloat16, jnp.float32
    return pl.pallas_call(
        functools.partial(layer_kernel, devices, per),
        out_shape=jax.ShapeDtypeStruct(shard, bf16),
        in_specs=[scalars, scalars, anywhere, anywhere, anywhere, anywhere],
        out_specs=pl.BlockSpec(memory_space=vmem),
        scratch_shapes=[
            vmem((full.shape[0] + 1, BLOCK, BLOCK), bf16),
            vmem((2 * count, width), bf16),
            vmem((width, RANK), bf16),
            vmem((RANK, width), bf16),
            vmem((width * RANK // (BLOCK * BLOCK) + 1, BLOCK, BLOCK), bf16),
            vmem((2 * count, RANK), f32),
            vmem((2 * count, RANK), bf16),
            vmem((2 * count, RANK), bf16),
            vmem((2 * count, BLOCK), f32),
            vmem((chips,) + shard, bf16),
            vmem((2 * depth,) + shard, bf16),
            vmem((depth,) + shard, bf16),
            vmem((depth - 1,) + shard, bf16),
            vmem(shard[1:], bf16),
            dma((3,)),
            dma((chips + 1,)),
            dma((2 * depth,)),
            dma((depth,)),
            dma((depth - 1,)),
            dma((2,)),
        ],
        compiler_params=pltpu.CompilerParams(
            collective_id=1, has_side_effects=True, vmem_limit_bytes=60 * 1024 * 1024
        ),
        name="layer_sums",
    )(places, begin, tokens, cotangent, other, full)


def one_section(tokens, blocks_in, blocks_out, pos_in, pos_out, cotangent):
    devices = lax.axis_size("dp")
    per = blocks_in.shape[1]
    places = jnp.concatenate([pos_in, pos_out]).astype(jnp.bfloat16)
    places = jnp.pad(places[:, None, :], ((0, 0), (0, EXTRA - 1), (0, BLOCK - per)))
    full, tags, other = gather_blocks(blocks_in[0], blocks_out[0], places, tokens, cotangent, devices)
    count = devices * per
    slots = tags[:, 0, :per].astype(jnp.int32)
    starts = per * jnp.arange(devices)[:, None] + jnp.arange(per)[None, :]
    numbers = jnp.arange((tokens.shape[1] // BLOCK) * (RANK // BLOCK))
    found = jnp.where(slots[None] == numbers[:, None, None], starts[None], count)
    begin = jnp.min(found, axis=(1, 2)).astype(jnp.int32)
    flat = full.reshape(count, BLOCK, BLOCK)
    sums = layer_sums(slots.reshape(-1), begin, tokens, cotangent, other, flat, devices, per)
    shape = blocks_in.shape
    return (sums[0].reshape(shape), sums[1].reshape(shape))


def solution(mesh):
    in_specs = (
        P("dp", None),
        P("section", "dp", None, None),
        P("section", "dp", None, None),
        P("section", "dp"),
        P("section", "dp"),
        P("dp", None),
    )
    out_specs = (P("section", "dp", None, None), P("section", "dp", None, None))
    body = one_section if mesh.shape["section"] == 1 else per_device
    return jax.shard_map(
        body, mesh=mesh, in_specs=in_specs, out_specs=out_specs, check_vma=False
    )
```

profile of v0, /device:TPU:1, one launch (start us, length us, event | category | flops | bytes accessed | tf_op | source)
XLA Modules:
  0.0 124.3 jit_solution(15410621892377549434)
XLA Ops:
  0.6 0.7 convert_bitcast_fusion
  1.3 0.6 fusion.5.own_tags
  1.9 55.6 %gather_blocks.1 = (bf16[32,5,128,128]{3,2,1,0:T(8,128)(2,1)}, bf16[32,16,128]{2,1,0:T(8,128)(2,1)}, bf16[128,8192]{1,0:T(8,128)(2,1)}) custom-call(bf16[5,128,128]{2,1,0:T(8,128)(2,1)} %bitcast.11, bf16[5,128,128]{2,1,0:T(8,128)(2,1)} %bitcast.12, bf16[2,16,128]{2,1,0:T(8,128)(2,1)} %fusion.5.own_tags, bf16[128,8192]{1,0:T(8,128)(2,1)} %tokens.3, ...), custom_call_target="tpu_custom_call" | custom-call | tf_op jit(solution)/shard_map/gather_blocks/pallas_call | solution.py:388
  57.5 0.9 fusion.6
  58.4 0.9 slice_convert_fusion
  59.2 0.7 reshape.74.pos
  59.9 0.1 copy.8
  60.0 0.7 select_reduce_fusion.begin
  60.7 61.9 %layer_sums.1 = bf16[2,640,128]{2,1,0:T(8,128)(2,1)} custom-call(s32[160]{0:T(256)} %reshape.74.pos, s32[256]{0:T(256)} %select_reduce_fusion.begin, bf16[128,8192]{1,0:T(8,128)(2,1)} %tokens.3, bf16[128,8192]{1,0:T(8,128)(2,1)} %cotangent.3, bf16[128,8192]{1,0:T(8,128)(2,1)} %get-tuple-element.6.other, bf16[160,128,128]{2,1,0:T(8,128)(2,1)} %bitcast.10), custom_call_target="tpu_custom_call" | custom-call | tf_op jit(solution)/shard_map/layer_sums/pallas_call | solution.py:587
  122.6 1.7 %fusion.7 = (bf16[1,640,128]{2,1,0:T(8,128)(2,1)}, bf16[1,640,128]{2,1,0:T(8,128)(2,1)}) fusion(bf16[2,640,128]{2,1,0:T(8,128)(2,1)} %layer_sums.1), kind=kLoop, calls=%fused_computation.16 | loop fusion | bytes 655360 | tf_op jit(solution)/shard_map/slice | solution.py:636
  (2 shorter events, 0.0 us)
where the time goes:
time: 125 us; the launch traced here: 124 us
  Pallas kernels  117 us (94%)
  other arithmetic  3.74 us (3%)
  local copies, waits for them, and re-layouts  2.48 us (2%)
    pallas_call x1, Pallas kernels, layer_sums(): pl.pallas_call(functools.partial(layer_kernel, devices, per), out_shape=j...  61.9 us
    pallas_call x1, Pallas kernels, gather_blocks(): pl.pallas_call(functools.partial(gather_kernel, devices), out_shape=(jax....  55.6 us

commit v1 on v0

v1 whole, which is shorter than its diff:
```python
import functools

import jax
import jax.numpy as jnp
from jax import lax
from jax.experimental import pallas as pl
from jax.experimental.pallas import tpu as pltpu
from jax.sharding import PartitionSpec as P

D = 8192
RANK = 512
BLOCK = 128
MICRO = 2


EPS = 1e-05


def from_behind(block, axis, distance):
    devices = range(lax.axis_size(axis))
    route = [(i - distance, i) for i in devices if i - distance in devices]
    return lax.ppermute(block, axis, route)


def expand(blocks, places, rows_b, cols_b):
    flat = jnp.zeros((rows_b * cols_b, BLOCK, BLOCK), blocks.dtype)
    flat = flat.at[places].set(blocks, mode="drop")
    return (
        flat.reshape(rows_b, cols_b, BLOCK, BLOCK)
        .transpose(0, 2, 1, 3)
        .reshape(rows_b * BLOCK, cols_b * BLOCK)
    )


def slot_grads(left, right, places, rows_b, cols_b):
    count = left.shape[0]
    valid = places < rows_b * cols_b
    row_block = jnp.where(valid, places // cols_b, 0).astype(jnp.int32)
    col_block = jnp.where(valid, places % cols_b, 0).astype(jnp.int32)
    left_blocks = jnp.take(left.reshape(count, rows_b, BLOCK), row_block, axis=1)
    right_blocks = jnp.take(right.reshape(count, cols_b, BLOCK), col_block, axis=1)
    result = jnp.einsum(
        "tjb,tjc->jbc", left_blocks, right_blocks, preferred_element_type=jnp.float32
    )
    return jnp.where(valid[:, None, None], result, 0.0)


def norm_parts(hidden):
    wide = hidden.astype(jnp.float32)
    scale = jnp.sqrt(jnp.mean(wide * wide, axis=-1, keepdims=True) + EPS)
    return (wide, scale)


def forward_layer(hidden, mat_a, mat_b):
    wide, scale = norm_parts(hidden)
    normed = (wide / scale).astype(jnp.bfloat16)
    pre = jnp.dot(normed, mat_a, preferred_element_type=jnp.float32)
    act = (pre * jax.nn.sigmoid(pre)).astype(jnp.bfloat16)
    return (wide + jnp.dot(act, mat_b, preferred_element_type=jnp.float32)).astype(jnp.bfloat16)


def backward_layer(hidden, upstream, mat_a, mat_b):
    wide, scale = norm_parts(hidden)
    unit = wide / scale
    normed = unit.astype(jnp.bfloat16)
    pre = jnp.dot(normed, mat_a, preferred_element_type=jnp.float32)
    sig = jax.nn.sigmoid(pre)
    act = (pre * sig).astype(jnp.bfloat16)
    dact = lax.dot_general(
        upstream, mat_b, (((1,), (1,)), ((), ())), preferred_element_type=jnp.float32
    )
    dpre = (dact * sig * (1.0 + pre * (1.0 - sig))).astype(jnp.bfloat16)
    dnorm = lax.dot_general(
        dpre, mat_a, (((1,), (1,)), ((), ())), preferred_element_type=jnp.float32
    )
    inner = jnp.mean(dnorm * unit, axis=-1, keepdims=True)
    earlier = (upstream.astype(jnp.float32) + (dnorm - unit * inner) / scale).astype(jnp.bfloat16)
    return (earlier, normed, dpre, act)


def store(stack, value, picked, active):
    updated = lax.dynamic_update_slice_in_dim(stack, value[None], picked, 0)
    return jnp.where(active, updated, stack)


def per_device(tokens, blocks_in, blocks_out, pos_in, pos_out, cotangent):
    sections = lax.axis_size("section")
    here = lax.axis_index("section")
    rows_d = D // BLOCK
    rows_k = RANK // BLOCK
    full_in, full_out, all_in, all_out = (
        lax.all_gather(blocks_in, "dp", axis=1, tiled=True),
        lax.all_gather(blocks_out, "dp", axis=1, tiled=True),
        lax.all_gather(pos_in, "dp", axis=1, tiled=True),
        lax.all_gather(pos_out, "dp", axis=1, tiled=True),
    )
    mat_a = expand(full_in[0], all_in[0], rows_d, rows_k)
    mat_b = expand(full_out[0], all_out[0], rows_k, rows_d)
    micro_rows = tokens.shape[0] // MICRO
    turns = MICRO + sections - 1
    saved = jnp.zeros((MICRO, micro_rows, D), jnp.bfloat16)
    carried = jnp.zeros((micro_rows, D), jnp.bfloat16)
    for turn in range(turns):
        micro = turn - here
        active = (micro >= 0) & (micro < MICRO)
        picked = jnp.clip(micro, 0, MICRO - 1)
        first = lax.dynamic_slice_in_dim(tokens, picked * micro_rows, micro_rows, 0)
        entering = jnp.where(here == 0, first, carried)
        saved = store(saved, entering, picked, active)
        if turn < turns - 1:
            leaving = lax.cond(
                active, lambda x: forward_layer(x, mat_a, mat_b), lambda x: x, entering
            )
            carried = from_behind(leaving, "section", 1)
    kept_normed = jnp.zeros((MICRO, micro_rows, D), jnp.bfloat16)
    kept_dpre = jnp.zeros((MICRO, micro_rows, RANK), jnp.bfloat16)
    kept_act = jnp.zeros((MICRO, micro_rows, RANK), jnp.bfloat16)
    kept_upper = jnp.zeros((MICRO, micro_rows, D), jnp.bfloat16)
    carried_grad = jnp.zeros((micro_rows, D), jnp.bfloat16)
    for turn in range(turns):
        micro = turn - (sections - 1 - here)
        active = (micro >= 0) & (micro < MICRO)
        picked = jnp.clip(micro, 0, MICRO - 1)
        last = lax.dynamic_slice_in_dim(cotangent, picked * micro_rows, micro_rows, 0)
        upstream = jnp.where(here == sections - 1, last, carried_grad)
        hidden = lax.dynamic_index_in_dim(saved, picked, 0, keepdims=False)

        def run_layer():
            return backward_layer(hidden, upstream, mat_a, mat_b)

        def skip_layer():
            return (
                upstream,
                jnp.zeros((micro_rows, D), jnp.bfloat16),
                jnp.zeros((micro_rows, RANK), jnp.bfloat16),
                jnp.zeros((micro_rows, RANK), jnp.bfloat16),
            )

        earlier, normed, dpre, act = lax.cond(active, run_layer, skip_layer)
        kept_normed = store(kept_normed, normed, picked, active)
        kept_dpre = store(kept_dpre, dpre, picked, active)
        kept_act = store(kept_act, act, picked, active)
        kept_upper = store(kept_upper, upstream, picked, active)
        if turn < turns - 1:
            carried_grad = from_behind(earlier, "section", -1)
    all_rows = MICRO * micro_rows
    terms_in = slot_grads(
        kept_normed.reshape(all_rows, D),
        kept_dpre.reshape(all_rows, RANK),
        all_in[0],
        rows_d,
        rows_k,
    )[None]
    terms_out = slot_grads(
        kept_act.reshape(all_rows, RANK),
        kept_upper.reshape(all_rows, D),
        all_out[0],
        rows_k,
        rows_d,
    )[None]
    sums_in, sums_out = (
        lax.psum_scatter(
            terms_in.astype(jnp.bfloat16), "dp", scatter_dimension=1, tiled=True
        ).astype(jnp.float32),
        lax.psum_scatter(
            terms_out.astype(jnp.bfloat16), "dp", scatter_dimension=1, tiled=True
        ).astype(jnp.float32),
    )
    return (sums_in.astype(jnp.bfloat16), sums_out.astype(jnp.bfloat16))


SLICES = 2
PLANE = 1
CHUNK = 1024


class Place:
    def __init__(self, devices):
        me = lax.axis_index("dp")
        self.depth = devices // 8
        self.me = me
        self.core = me % 2
        self.chip = me // 2
        x = self.chip % 2
        y = (self.chip // 2) % 2
        self.z = self.chip // 4
        dx = 1 - 2 * x
        dy = 2 * (1 - 2 * y)
        first = (1 - self.core) * dx + self.core * dy
        second = (1 - self.core) * dy + self.core * dx
        self.own = self.chip % 4
        self.near = self.own + first
        self.far = self.own + second
        self.diag = self.own + first + second
        self.sibling = me + 1 - 2 * self.core
        self.first = me + 2 * first
        self.second = me + 2 * second
        self.above = me + 8
        self.below = me - 8
        self.has_above = self.z + 1 < self.depth
        self.has_below = self.z >= 1

    def knock(self):
        barrier = pltpu.get_barrier_semaphore()

        def signal(peer):
            pl.semaphore_signal(
                barrier, inc=1, device_id={"dp": peer}, device_id_type=pl.DeviceIdType.MESH
            )

        for peer in (self.sibling, self.first, self.second):
            signal(peer)
        pl.when(self.has_above)(lambda: signal(self.above))
        pl.when(self.has_below)(lambda: signal(self.below))

        peers = 3 + self.has_above.astype(jnp.int32) + self.has_below.astype(jnp.int32)
        return lambda: pl.semaphore_wait(barrier, peers)


def remote(src, dst, send, recv, peer):
    return pltpu.make_async_remote_copy(
        src_ref=src,
        dst_ref=dst,
        send_sem=send,
        recv_sem=recv,
        device_id={"dp": peer},
        device_id_type=pl.DeviceIdType.MESH,
    )


class Layout:
    def __init__(self, devices, per):
        self.per = per
        self.depth = devices // 8
        self.sizes = (4 * (per - PLANE), 4 * PLANE)
        self.plane = 16 * per
        self.total = self.depth * self.plane

    def start(self, part, z, p):
        line, odd = self.sizes
        return z * self.plane + (p * line if part == 0 else 4 * line + p * odd)

    def piece(self, buf, k, part, z, p):
        span = pl.ds(self.start(part, z, p), self.sizes[part])
        return buf.at[span] if k is None else buf.at[k, span]

    def level(self, buf, k, z):
        line, odd = self.sizes
        span = pl.ds(z * self.plane + 4 * line, 4 * odd)
        return buf.at[span] if k is None else buf.at[k, span]


def fused_kernel(devices, pos_in, pos_out, own_in, own_out, tokens, cotangent, out_in, out_out,
                 full, stage, rows_h, rows_g, mats, grads, inverse,
                 tags, table, table_s, begin, begin_s, mid,
                 held, from_second, from_first, from_below, from_above, final, twin, flat,
                 load_sems, send_sems, pair_sems, twin_sems, tag_sems, gather_sems, level_sems,
                 second_sems, first_sems, below_sems, above_sems):
    at = Place(devices)
    depth = at.depth
    core = at.core
    per = own_in.shape[0]
    lay = Layout(devices, per)
    count, width = tokens.shape
    size = full[0].shape[1]
    half = BLOCK // 2
    rows_k = RANK // BLOCK
    rows_d = width // BLOCK
    blocks = rows_k * rows_d
    ranks = rows_k * size
    chunks = width // CHUNK
    sends = []

    def send(src, dst, recv, peer, present=None):
        remote(src, dst, send_sems.at[len(sends)], recv, peer).start()
        rows, whole = src.shape[0], src.dtype == jnp.int32
        if whole and len(src.shape) == 2:
            sends.append((lambda: tags.at[0], present))
        elif whole:
            sends.append((lambda: tags.at[pl.ds(0, rows)], present))
        else:
            sends.append((lambda: full[0].at[pl.ds(0, rows)], present))

    def got(buf, sem):
        remote(buf, buf, send_sems.at[0], sem, at.sibling).wait_recv()

    wait_peers = at.knock()

    own_rows = pl.ds(pl.multiple_of(core * count, count), count)
    local = [
        pltpu.make_async_copy(tokens, rows_h.at[own_rows], load_sems.at[0]),
        pltpu.make_async_copy(cotangent, rows_g.at[own_rows], load_sems.at[1]),
    ]
    for copy in local:
        copy.start()

    def offset(part, j):
        return 2 * j if part == 0 else 2 * (j - (per - PLANE))

    def part_of(j):
        return 0 if j < per - PLANE else 1

    lanes = lax.broadcasted_iota(jnp.int32, tags.shape[1:], 1)
    row = jnp.full(tags.shape[1:], blocks, jnp.int32)
    for j in range(per):
        row = jnp.where(lanes == 2 * j, pos_in[0, j], row)
        row = jnp.where(lanes == 2 * j + 1, pos_out[0, j] + blocks + 1, row)
    tags[at.me] = row

    for j in range(per):
        part = part_of(j)
        base = lay.start(part, at.z, at.own) + core * (lay.sizes[part] // 2) + offset(part, j)
        flat[0] = own_in[j].T
        flat[1] = own_out[j]
        for k in range(SLICES):
            keep = pl.ds(pl.multiple_of(core * half + k * size, size), size)
            give = pl.ds(pl.multiple_of((1 - core) * half + k * size, size), size)
            for m in range(2):
                full[k][base + m] = flat[m, keep, :]
                stage[k, 2 * j + m] = flat[m, give, :]
    for k in range(SLICES):
        full[k][lay.total] = jnp.zeros((size, BLOCK), jnp.bfloat16)
        for m in range(2):
            grads[k][m * (blocks + 1) + blocks] = jnp.zeros((size, BLOCK), jnp.bfloat16)

    wait_peers()

    def pair(k, start):
        for part in range(2):
            n = lay.sizes[part] // 2
            base = lay.start(part, at.z, at.own) + core * n
            first = 0 if part == 0 else lay.sizes[0] // 2
            src, dst = stage.at[k, pl.ds(first, n)], full[k].at[pl.ds(base, n)]
            if start:
                send(src, dst, pair_sems.at[k, part], at.sibling)
            else:
                got(src, pair_sems.at[k, part])

    send(tags.at[at.me], tags.at[at.me], tag_sems.at[2 * depth * 4], at.sibling)
    for k in range(SLICES):
        pair(k, True)

    def tag_piece(z, p):
        return tags.at[pl.ds(2 * (4 * z + p), 2)]

    def push(k, part, z, p, peer, present=None):
        if k == 0 and part == 0:
            piece = tag_piece(z, p)
            send(piece, piece, tag_sems.at[4 * z + p], peer, present)
        piece = lay.piece(full[k], None, part, z, p)
        send(piece, piece, gather_sems.at[k, part, 4 * z + p], peer, present)

    def arrived(k, part, z, p):
        if k == 0 and part == 0:
            got(tag_piece(z, p), tag_sems.at[4 * z + p])
        got(lay.piece(full[k], None, part, z, p), gather_sems.at[k, part, 4 * z + p])

    def when(cond, run):
        pl.when(cond)(run)

    def up_push(k, z, p, present):
        when(at.has_above, lambda: push(k, 0, z, p, at.above, present))

    def down_push(k, z, p, present):
        when(at.has_below, lambda: push(k, 0, z, p, at.below, present))

    def gather_own(k):
        pair(k, False)
        if k == 0:
            got(tags.at[at.me], tag_sems.at[2 * depth * 4])
        push(k, 0, at.z, at.own, at.second)
        push(k, 0, at.z, at.own, at.first)
        up_push(k, at.z, at.own, lambda: at.has_above)
        down_push(k, at.z, at.own, lambda: at.has_below)
        push(k, 1, at.z, at.own, at.second)
        push(k, 1, at.z, at.own, at.first)

    def near_own(k):
        for part in range(2):
            arrived(k, part, at.z, at.near)
            push(k, part, at.z, at.near, at.second)

    def line(k, d):
        def below():
            z = at.z - d
            arrived(k, 0, z, at.own)
            up_push(k, z, at.own, lambda: at.has_above & (at.z >= d))
            push(k, 0, z, at.own, at.second, lambda: at.z >= d)
            push(k, 0, z, at.own, at.first, lambda: at.z >= d)

        def above():
            z = at.z + d
            arrived(k, 0, z, at.own)
            down_push(k, z, at.own, lambda: at.has_below & (at.z + d < depth))
            push(k, 0, z, at.own, at.second, lambda: at.z + d < depth)
            push(k, 0, z, at.own, at.first, lambda: at.z + d < depth)

        when(at.z >= d, below)
        when(at.z + d < depth, above)

    def near_line(k, d):
        def below():
            arrived(k, 0, at.z - d, at.near)
            push(k, 0, at.z - d, at.near, at.second, lambda: at.z >= d)

        def above():
            arrived(k, 0, at.z + d, at.near)
            push(k, 0, at.z + d, at.near, at.second, lambda: at.z + d < depth)

        when(at.z >= d, below)
        when(at.z + d < depth, above)

    def push_level(k, z, peer, to_above, present):
        piece = lay.level(full[k], None, z)
        send(piece, piece, level_sems.at[k, z], peer, present)

    def plane_own(k):
        for part in range(2):
            for p in (at.far, at.diag):
                arrived(k, part, at.z, p)
        when(at.has_above, lambda: push_level(k, at.z, at.above, True, lambda: at.has_above))
        when(at.has_below, lambda: push_level(k, at.z, at.below, False, lambda: at.has_below))

    def plane(k, d):
        def below():
            got(lay.level(full[k], None, at.z - d), level_sems.at[k, at.z - d])
            when(
                at.has_above,
                lambda: push_level(k, at.z - d, at.above, True, lambda: at.has_above & (at.z >= d)),
            )

        def above():
            got(lay.level(full[k], None, at.z + d), level_sems.at[k, at.z + d])
            when(
                at.has_below,
                lambda: push_level(
                    k, at.z + d, at.below, False, lambda: at.has_below & (at.z + d < depth)
                ),
            )

        when(at.z >= d, below)
        when(at.z + d < depth, above)

    def side(k):
        for d in range(1, depth):

            def below(d=d):
                for p in (at.far, at.diag):
                    arrived(k, 0, at.z - d, p)

            def above(d=d):
                for p in (at.far, at.diag):
                    arrived(k, 0, at.z + d, p)

            when(at.z >= d, below)
            when(at.z + d < depth, above)

    def load_rows():
        swap = [
            remote(tokens, rows_h.at[own_rows], send_sems.at[len(sends)], load_sems.at[2], at.sibling),
            remote(cotangent, rows_g.at[own_rows], send_sems.at[len(sends) + 1], load_sems.at[3], at.sibling),
        ]
        for copy, src in zip(swap, (tokens, cotangent)):
            copy.start()
            sends.append((lambda src=src: src, None))
        return swap

    def scales():
        total = jnp.zeros((2 * count, BLOCK), jnp.float32)
        for i in range(0, width, BLOCK):
            wide = rows_h[:, i : i + BLOCK].astype(jnp.float32)
            total += wide * wide
        scale = jnp.sqrt(jnp.sum(total, axis=-1, keepdims=True) / width + EPS)
        inverse[...] = jnp.broadcast_to(1.0 / scale, inverse.shape)

    def tables():
        table[...] = tags[:, 0, :]
        copy = pltpu.make_async_copy(table, table_s, load_sems.at[4])
        copy.start()
        copy.wait()
        shape = begin.shape
        numbers = lax.broadcasted_iota(jnp.int32, shape, 0) * BLOCK
        numbers += lax.broadcasted_iota(jnp.int32, shape, 1)

        def scan(dev, found):
            z, p, which = dev // 8, (dev // 2) % 4, dev % 2
            for lane in range(2 * per):
                part = part_of(lane // 2)
                first = 0 if part == 0 else lay.sizes[0] // 2
                entry = lay.start(part, z, p) + which * (lay.sizes[part] // 2) + lane - first
                found = jnp.where(numbers == table_s[dev, lane], entry, found)
            return found

        begin[...] = lax.fori_loop(0, devices, scan, jnp.full(shape, lay.total, jnp.int32))
        copy = pltpu.make_async_copy(begin, begin_s, load_sems.at[4])
        copy.start()
        copy.wait()

    def expand(k, m):
        def step(r, carry):
            into = pl.ds(pl.multiple_of(r * BLOCK, BLOCK), BLOCK)
            for c in range(rows_k):
                b = r * rows_k + c if m == 0 else blocks + 1 + c * rows_d + r
                mats[m, c * size : (c + 1) * size, into] = full[k][begin_s[b // BLOCK, b % BLOCK]]
            return carry

        lax.fori_loop(0, rows_d, step, 0)

    def product(m):
        rows = rows_h if m == 0 else rows_g
        total = jnp.zeros((2 * count, ranks), jnp.float32)
        for i in range(0, width, CHUNK):
            total += lax.dot_general(
                rows[:, i : i + CHUNK], mats[m, :, i : i + CHUNK],
                (((1,), (1,)), ((), ())), preferred_element_type=jnp.float32,
            )
        return total

    def middle(k):
        pre = product(0) * inverse[:, :1]
        dact = product(1)
        sig = jax.nn.sigmoid(pre)
        dpre = dact * sig * (1.0 + pre * (1.0 - sig))
        mid[0] = (dpre * inverse[:, :1]).astype(jnp.bfloat16)
        mid[1] = (pre * sig).astype(jnp.bfloat16)

    def outer(k, m):
        rows = rows_h if m == 0 else rows_g

        def step(i, carry):
            into = pl.ds(pl.multiple_of(i * CHUNK, CHUNK), CHUNK)
            part = lax.dot_general(
                mid[m], rows[:, into], (((0,), (0,)), ((), ())), preferred_element_type=jnp.float32
            ).astype(jnp.bfloat16)
            for r in range(CHUNK // BLOCK):
                col = i * (CHUNK // BLOCK) + r
                for c in range(rows_k):
                    b = col * rows_k + c if m == 0 else blocks + 1 + c * rows_d + col
                    grads[k][b] = part[c * size : (c + 1) * size, r * BLOCK : (r + 1) * BLOCK]
            return carry

        lax.fori_loop(0, chunks, step, 0)

    def fill(k, part, z, p, terms, into=None):
        n = lay.sizes[part] // 2
        first = 0 if part == 0 else lay.sizes[0] // 2
        target = held if into is None else into
        base = lay.start(part, z, p)

        def step(which, carry):
            dev = 2 * (4 * z + p) + which
            for i in range(n):
                entry = base + which * n + i
                value = grads[k][table_s[dev, first + i]]
                if terms:
                    value = value.astype(jnp.float32)
                    for term in terms:
                        value += term[k, entry].astype(jnp.float32)
                    value = value.astype(jnp.bfloat16)
                if into is None:
                    target[k, entry] = value
                else:
                    target[k, 2 * first + which * n + i] = value
            return carry

        lax.fori_loop(0, 2, step, 0)

    def give(k, part, z, p, buf, sems, peer, present=None):
        src = lay.piece(held, k, part, z, p)
        send(src, lay.piece(buf, k, part, z, p), sems.at[k, part, 4 * z + p], peer, present)

    def take(k, part, z, p, buf, sems):
        got(lay.piece(buf, k, part, z, p), sems.at[k, part, 4 * z + p])

    def reduce_levels(k):
        for d in range(depth - 1, 0, -1):

            def upward(d=d):
                z = at.z + d

                def own():
                    for p in range(4):
                        fill(k, 1, z, p, [])

                def summed():
                    got(lay.level(from_below, k, z), below_sems.at[k, 1, z])
                    for p in range(4):
                        fill(k, 1, z, p, [from_below])

                when(jnp.logical_not(at.has_below), own)
                when(at.has_below, summed)
                send(
                    lay.level(held, k, z), lay.level(from_below, k, z), below_sems.at[k, 1, z],
                    at.above, lambda: at.z + d < depth,
                )

            def downward(d=d):
                z = at.z - d

                def own():
                    for p in range(4):
                        fill(k, 1, z, p, [])

                def summed():
                    got(lay.level(from_above, k, z), above_sems.at[k, 1, z])
                    for p in range(4):
                        fill(k, 1, z, p, [from_above])

                when(jnp.logical_not(at.has_above), own)
                when(at.has_above, summed)
                send(
                    lay.level(held, k, z), lay.level(from_above, k, z), above_sems.at[k, 1, z],
                    at.below, lambda: at.z >= d,
                )

            when(at.z + d < depth, upward)
            when(at.z >= d, downward)

    def beside(run):
        when(at.has_below & at.has_above, lambda: run([from_below, from_above]))
        when(at.has_below & jnp.logical_not(at.has_above), lambda: run([from_below]))
        when(at.has_above & jnp.logical_not(at.has_below), lambda: run([from_above]))

    def order():
        return [(at.z + d) % depth for d in (2, 1, 3, 0)][-depth:] if depth == 4 else [
            (at.z + d) % depth for d in range(depth - 1, -1, -1)
        ]

    def reduce_second(k):
        for z in order():
            for p in (at.diag, at.far):
                fill(k, 0, z, p, [])
                give(k, 0, z, p, from_second, second_sems, at.second)

    def level_sums(k):
        when(at.has_below, lambda: got(lay.level(from_below, k, at.z), below_sems.at[k, 1, at.z]))
        when(at.has_above, lambda: got(lay.level(from_above, k, at.z), above_sems.at[k, 1, at.z]))

        def run(terms):
            for p in (at.diag, at.far):
                fill(k, 1, at.z, p, terms)

        beside(run)
        for p in (at.diag, at.far):
            give(k, 1, at.z, p, from_second, second_sems, at.second)

    def reduce_first(k):
        for z in order():
            take(k, 0, z, at.near, from_second, second_sems)
            fill(k, 0, z, at.near, [from_second])
            give(k, 0, z, at.near, from_first, first_sems, at.first)

    def level_first(k):
        take(k, 1, at.z, at.near, from_second, second_sems)
        beside(lambda terms: fill(k, 1, at.z, at.near, [from_second] + terms))
        give(k, 1, at.z, at.near, from_first, first_sems, at.first)

    def reduce_line(k):
        terms = [from_second, from_first]
        for d in range(depth - 1, 0, -1):

            def upward(d=d):
                z = at.z + d
                take(k, 0, z, at.own, from_second, second_sems)
                take(k, 0, z, at.own, from_first, first_sems)
                when(jnp.logical_not(at.has_below), lambda: fill(k, 0, z, at.own, terms))

                def summed():
                    take(k, 0, z, at.own, from_below, below_sems)
                    fill(k, 0, z, at.own, terms + [from_below])

                when(at.has_below, summed)
                give(k, 0, z, at.own, from_below, below_sems, at.above, lambda: at.z + d < depth)

            def downward(d=d):
                z = at.z - d
                take(k, 0, z, at.own, from_second, second_sems)
                take(k, 0, z, at.own, from_first, first_sems)
                when(jnp.logical_not(at.has_above), lambda: fill(k, 0, z, at.own, terms))

                def summed():
                    take(k, 0, z, at.own, from_above, above_sems)
                    fill(k, 0, z, at.own, terms + [from_above])

                when(at.has_above, summed)
                give(k, 0, z, at.own, from_above, above_sems, at.below, lambda: at.z >= d)

            when(at.z + d < depth, upward)
            when(at.z >= d, downward)

    def finish(k):
        for part in (1, 0):
            take(k, part, at.z, at.own, from_second, second_sems)
            take(k, part, at.z, at.own, from_first, first_sems)
        when(at.has_below, lambda: take(k, 0, at.z, at.own, from_below, below_sems))
        when(at.has_above, lambda: take(k, 0, at.z, at.own, from_above, above_sems))

        def run(terms):
            for part in range(2):
                fill(k, part, at.z, at.own, [from_second, from_first] + terms, final)

        beside(run)
        for part in range(2):
            n = lay.sizes[part] // 2
            first = 0 if part == 0 else lay.sizes[0]
            piece = pl.ds(first + (1 - core) * n, n)
            send(final.at[k, piece], twin.at[k, piece], twin_sems.at[k, part], at.sibling)

    def assemble(k):
        for part in range(2):
            n = lay.sizes[part] // 2
            first = 0 if part == 0 else lay.sizes[0]
            piece = pl.ds(first + core * n, n)
            got(twin.at[k, piece], twin_sems.at[k, part])
        for j in range(per):
            part = part_of(j)
            first = 0 if part == 0 else lay.sizes[0]
            entry = first + core * (lay.sizes[part] // 2) + offset(part, j)
            mine = pl.ds(pl.multiple_of(core * half + k * size, size), size)
            theirs = pl.ds(pl.multiple_of((1 - core) * half + k * size, size), size)
            flat[j, mine, :] = final[k, entry]
            flat[j, theirs, :] = twin[k, entry]
            out_out[j, mine, :] = final[k, entry + 1]
            out_out[j, theirs, :] = twin[k, entry + 1]

    swap = None
    gather_own(0)
    swap = load_rows()
    near_own(0)
    line(0, 1)
    line(0, 2) if depth > 2 else None
    near_line(0, 1)
    plane_own(0)
    for d in range(3, depth):
        line(0, d)
    for d in range(2, depth):
        near_line(0, d)
        plane(0, d - 1)
    plane(0, depth - 1)
    for k in range(1, SLICES):
        gather_own(k)
    for copy in local:
        copy.wait()
    for copy in swap:
        copy.wait_recv()
    scales()
    side(0)
    tables()
    for k in range(SLICES):
        more = k + 1 < SLICES
        expand(k, 0)
        if more:
            near_own(k + 1)
            line(k + 1, 1)
        expand(k, 1)
        middle(k)
        if more:
            for d in range(2, depth):
                line(k + 1, d)
            near_line(k + 1, 1)
            plane_own(k + 1)
        outer(k, 0)
        if more:
            for d in range(2, depth):
                near_line(k + 1, d)
            for d in range(1, depth):
                plane(k + 1, d)
        outer(k, 1)
        reduce_levels(k)
        reduce_second(k)
        if more:
            side(k + 1)
        else:
            for k in range(SLICES):
                reduce_first(k)
                level_sums(k)
                level_first(k)
                reduce_line(k)
                finish(k)
    for k in range(SLICES):
        assemble(k)
    for j in range(per):
        out_in[j] = flat[j].T
    for n, (like, present) in enumerate(sends):

        def sent(n=n, like=like):
            remote(like(), like(), send_sems.at[n], load_sems.at[0], at.sibling).wait_send()

        if present is None:
            sent()
        else:
            pl.when(present())(sent)


def one_section(tokens, blocks_in, blocks_out, pos_in, pos_out, cotangent):
    devices = lax.axis_size("dp")
    per = blocks_in.shape[1]
    count, width = tokens.shape
    lay = Layout(devices, per)
    depth = lay.depth
    chips = devices // 2
    size = BLOCK // 2 // SLICES
    ranks = RANK // BLOCK * size
    blocks = (width // BLOCK) * (RANK // BLOCK)
    dma = pltpu.SemaphoreType.DMA
    vmem = pltpu.VMEM
    anywhere = pl.BlockSpec(memory_space=pl.ANY)
    scalars = pl.BlockSpec(memory_space=pltpu.SMEM)
    local = pl.BlockSpec(memory_space=vmem)
    bf16, f32, i32 = jnp.bfloat16, jnp.float32, jnp.int32
    shards = (SLICES, lay.total, size, BLOCK)
    words = -(-2 * (blocks + 1) // BLOCK)
    words = -(-words // 8) * 8
    out = jax.ShapeDtypeStruct((per, BLOCK, BLOCK), bf16)
    results = pl.pallas_call(
        functools.partial(fused_kernel, devices),
        out_shape=(out, out),
        in_specs=[scalars, scalars, local, local, anywhere, anywhere],
        out_specs=(local, local),
        scratch_shapes=[
            [vmem((lay.total + 1, size, BLOCK), bf16) for _ in range(SLICES)],
            vmem((SLICES, 2 * per, size, BLOCK), bf16),
            vmem((2 * count, width), bf16),
            vmem((2 * count, width), bf16),
            vmem((2, ranks, width), bf16),
            [vmem((2 * (blocks + 1), size, BLOCK), bf16) for _ in range(SLICES)],
            vmem((2 * count, BLOCK), f32),
            vmem((devices, 8, BLOCK), i32),
            vmem((devices, BLOCK), i32),
            pltpu.SMEM((devices, BLOCK), i32),
            vmem((words, BLOCK), i32),
            pltpu.SMEM((words, BLOCK), i32),
            vmem((2, 2 * count, ranks), bf16),
            vmem(shards, bf16),
            vmem(shards, bf16),
            vmem(shards, bf16),
            vmem(shards, bf16),
            vmem(shards, bf16),
            vmem((SLICES, 4 * per, size, BLOCK), bf16),
            vmem((SLICES, 4 * per, size, BLOCK), bf16),
            vmem((per, BLOCK, BLOCK), bf16),
            dma((5,)),
            dma((400,)),
            dma((SLICES, 2)),
            dma((SLICES, 2)),
            dma((chips + 1 + chips,)),
            dma((SLICES, 2, chips)),
            dma((SLICES, depth)),
            dma((SLICES, 2, chips)),
            dma((SLICES, 2, chips)),
            dma((SLICES, 2, chips)),
            dma((SLICES, 2, chips)),
        ],
        compiler_params=pltpu.CompilerParams(
            collective_id=0, has_side_effects=True, vmem_limit_bytes=63 * 1024 * 1024
        ),
        name="fused_adapters",
    )(pos_in, pos_out, blocks_in[0], blocks_out[0], tokens, cotangent)
    return (results[0][None], results[1][None])


def solution(mesh):
    in_specs = (
        P("dp", None),
        P("section", "dp", None, None),
        P("section", "dp", None, None),
        P("section", "dp"),
        P("section", "dp"),
        P("dp", None),
    )
    out_specs = (P("section", "dp", None, None), P("section", "dp", None, None))
    body = one_section if mesh.shape["section"] == 1 else per_device
    return jax.shard_map(
        body, mesh=mesh, in_specs=in_specs, out_specs=out_specs, check_vma=False
    )
```

time: 125 us -> 139 us (1.11)
  Pallas kernels: 117 us -> 135 us
  other arithmetic: 3.74 us -> 0 us
    pallas_call x2 -> x1, Pallas kernels: 117 us -> 135 us  [one_section(): pl.pallas_call(functools.partial(fused_kernel, devices), out_shape=(out,...]
    unnamed x0 -> x2, local copies, waits for them, and re-layouts: none -> 3.19 us
    convert_element_type x2 -> x0, other arithmetic: 1.75 us -> none  [one_section(): slots = tags[:, 0, :per].astype(jnp.int32)]
    slice x1 -> x0, local copies, waits for them, and re-layouts: 1.74 us -> none  [one_section(): return (sums[0].reshape(shape), sums[1].reshape(shape))]
where the time goes in v1:
time: 139 us
  Pallas kernels  135 us (97%)
  local copies, waits for them, and re-layouts  3.19 us (2%)
    pallas_call x1, Pallas kernels, one_section(): pl.pallas_call(functools.partial(fused_kernel, devices), out_shape=(out,...  135 us
    unnamed x2, local copies, waits for them, and re-layouts  3.19 us

profile of v1, /device:TPU:1, one launch (start us, length us, event | category | flops | bytes accessed | tf_op | source)
XLA Modules:
  0.0 138.8 jit_solution(11431036951214086003)
XLA Ops:
  0.6 134.9 %fused_adapters.1 = (bf16[5,128,128]{2,1,0:T(8,128)(2,1)}, bf16[5,128,128]{2,1,0:T(8,128)(2,1)}) custom-call(s32[1,5]{1,0:T(1,128)} %pos_in.1, s32[1,5]{1,0:T(1,128)} %pos_out.1, bf16[5,128,128]{2,1,0:T(8,128)(2,1)} %bitcast.4, bf16[5,128,128]{2,1,0:T(8,128)(2,1)} %bitcast.5, bf16[128,8192]{1,0:T(8,128)(2,1)} %tokens.1, bf16[128,8192]{1,0:T(8,128)(2,1)} %cotangent.1), custom_call_target="tpu_custom_call" | custom-call | tf_op jit(solution)/shard_map/fused_adapters/pallas_call | solution.py:815
  135.6 1.6 %copy.10 = bf16[1,5,128,128]{3,2,1,0:T(8,128)(2,1)} copy(bf16[1,5,128,128]{3,2,1,0:T(8,128)(2,1)} %bitcast.7) | data formatting | bytes 327680
  137.2 1.6 %copy.11 = bf16[1,5,128,128]{3,2,1,0:T(8,128)(2,1)} copy(bf16[1,5,128,128]{3,2,1,0:T(8,128)(2,1)} %bitcast.6) | data formatting | bytes 327680

commit v2 on v1

v2 whole, which is shorter than its diff:
```python
import functools

import jax
import jax.numpy as jnp
from jax import lax
from jax.experimental import pallas as pl
from jax.experimental.pallas import tpu as pltpu
from jax.sharding import PartitionSpec as P

D = 8192
RANK = 512
BLOCK = 128
MICRO = 2


EPS = 1e-05


def from_behind(block, axis, distance):
    devices = range(lax.axis_size(axis))
    route = [(i - distance, i) for i in devices if i - distance in devices]
    return lax.ppermute(block, axis, route)


def expand(blocks, places, rows_b, cols_b):
    flat = jnp.zeros((rows_b * cols_b, BLOCK, BLOCK), blocks.dtype)
    flat = flat.at[places].set(blocks, mode="drop")
    return (
        flat.reshape(rows_b, cols_b, BLOCK, BLOCK)
        .transpose(0, 2, 1, 3)
        .reshape(rows_b * BLOCK, cols_b * BLOCK)
    )


def slot_grads(left, right, places, rows_b, cols_b):
    count = left.shape[0]
    valid = places < rows_b * cols_b
    row_block = jnp.where(valid, places // cols_b, 0).astype(jnp.int32)
    col_block = jnp.where(valid, places % cols_b, 0).astype(jnp.int32)
    left_blocks = jnp.take(left.reshape(count, rows_b, BLOCK), row_block, axis=1)
    right_blocks = jnp.take(right.reshape(count, cols_b, BLOCK), col_block, axis=1)
    result = jnp.einsum(
        "tjb,tjc->jbc", left_blocks, right_blocks, preferred_element_type=jnp.float32
    )
    return jnp.where(valid[:, None, None], result, 0.0)


def norm_parts(hidden):
    wide = hidden.astype(jnp.float32)
    scale = jnp.sqrt(jnp.mean(wide * wide, axis=-1, keepdims=True) + EPS)
    return (wide, scale)


def forward_layer(hidden, mat_a, mat_b):
    wide, scale = norm_parts(hidden)
    normed = (wide / scale).astype(jnp.bfloat16)
    pre = jnp.dot(normed, mat_a, preferred_element_type=jnp.float32)
    act = (pre * jax.nn.sigmoid(pre)).astype(jnp.bfloat16)
    return (wide + jnp.dot(act, mat_b, preferred_element_type=jnp.float32)).astype(jnp.bfloat16)


def backward_layer(hidden, upstream, mat_a, mat_b):
    wide, scale = norm_parts(hidden)
    unit = wide / scale
    normed = unit.astype(jnp.bfloat16)
    pre = jnp.dot(normed, mat_a, preferred_element_type=jnp.float32)
    sig = jax.nn.sigmoid(pre)
    act = (pre * sig).astype(jnp.bfloat16)
    dact = lax.dot_general(
        upstream, mat_b, (((1,), (1,)), ((), ())), preferred_element_type=jnp.float32
    )
    dpre = (dact * sig * (1.0 + pre * (1.0 - sig))).astype(jnp.bfloat16)
    dnorm = lax.dot_general(
        dpre, mat_a, (((1,), (1,)), ((), ())), preferred_element_type=jnp.float32
    )
    inner = jnp.mean(dnorm * unit, axis=-1, keepdims=True)
    earlier = (upstream.astype(jnp.float32) + (dnorm - unit * inner) / scale).astype(jnp.bfloat16)
    return (earlier, normed, dpre, act)


def store(stack, value, picked, active):
    updated = lax.dynamic_update_slice_in_dim(stack, value[None], picked, 0)
    return jnp.where(active, updated, stack)


def per_device(tokens, blocks_in, blocks_out, pos_in, pos_out, cotangent):
    sections = lax.axis_size("section")
    here = lax.axis_index("section")
    rows_d = D // BLOCK
    rows_k = RANK // BLOCK
    full_in, full_out, all_in, all_out = (
        lax.all_gather(blocks_in, "dp", axis=1, tiled=True),
        lax.all_gather(blocks_out, "dp", axis=1, tiled=True),
        lax.all_gather(pos_in, "dp", axis=1, tiled=True),
        lax.all_gather(pos_out, "dp", axis=1, tiled=True),
    )
    mat_a = expand(full_in[0], all_in[0], rows_d, rows_k)
    mat_b = expand(full_out[0], all_out[0], rows_k, rows_d)
    micro_rows = tokens.shape[0] // MICRO
    turns = MICRO + sections - 1
    saved = jnp.zeros((MICRO, micro_rows, D), jnp.bfloat16)
    carried = jnp.zeros((micro_rows, D), jnp.bfloat16)
    for turn in range(turns):
        micro = turn - here
        active = (micro >= 0) & (micro < MICRO)
        picked = jnp.clip(micro, 0, MICRO - 1)
        first = lax.dynamic_slice_in_dim(tokens, picked * micro_rows, micro_rows, 0)
        entering = jnp.where(here == 0, first, carried)
        saved = store(saved, entering, picked, active)
        if turn < turns - 1:
            leaving = lax.cond(
                active, lambda x: forward_layer(x, mat_a, mat_b), lambda x: x, entering
            )
            carried = from_behind(leaving, "section", 1)
    kept_normed = jnp.zeros((MICRO, micro_rows, D), jnp.bfloat16)
    kept_dpre = jnp.zeros((MICRO, micro_rows, RANK), jnp.bfloat16)
    kept_act = jnp.zeros((MICRO, micro_rows, RANK), jnp.bfloat16)
    kept_upper = jnp.zeros((MICRO, micro_rows, D), jnp.bfloat16)
    carried_grad = jnp.zeros((micro_rows, D), jnp.bfloat16)
    for turn in range(turns):
        micro = turn - (sections - 1 - here)
        active = (micro >= 0) & (micro < MICRO)
        picked = jnp.clip(micro, 0, MICRO - 1)
        last = lax.dynamic_slice_in_dim(cotangent, picked * micro_rows, micro_rows, 0)
        upstream = jnp.where(here == sections - 1, last, carried_grad)
        hidden = lax.dynamic_index_in_dim(saved, picked, 0, keepdims=False)

        def run_layer():
            return backward_layer(hidden, upstream, mat_a, mat_b)

        def skip_layer():
            return (
                upstream,
                jnp.zeros((micro_rows, D), jnp.bfloat16),
                jnp.zeros((micro_rows, RANK), jnp.bfloat16),
                jnp.zeros((micro_rows, RANK), jnp.bfloat16),
            )

        earlier, normed, dpre, act = lax.cond(active, run_layer, skip_layer)
        kept_normed = store(kept_normed, normed, picked, active)
        kept_dpre = store(kept_dpre, dpre, picked, active)
        kept_act = store(kept_act, act, picked, active)
        kept_upper = store(kept_upper, upstream, picked, active)
        if turn < turns - 1:
            carried_grad = from_behind(earlier, "section", -1)
    all_rows = MICRO * micro_rows
    terms_in = slot_grads(
        kept_normed.reshape(all_rows, D),
        kept_dpre.reshape(all_rows, RANK),
        all_in[0],
        rows_d,
        rows_k,
    )[None]
    terms_out = slot_grads(
        kept_act.reshape(all_rows, RANK),
        kept_upper.reshape(all_rows, D),
        all_out[0],
        rows_k,
        rows_d,
    )[None]
    sums_in, sums_out = (
        lax.psum_scatter(
            terms_in.astype(jnp.bfloat16), "dp", scatter_dimension=1, tiled=True
        ).astype(jnp.float32),
        lax.psum_scatter(
            terms_out.astype(jnp.bfloat16), "dp", scatter_dimension=1, tiled=True
        ).astype(jnp.float32),
    )
    return (sums_in.astype(jnp.bfloat16), sums_out.astype(jnp.bfloat16))


SLICES = 2
GATHER_PLANE = (1, 1)
REDUCE_PLANE = (1, 1)
CHUNK = 1024

def plain_order(depth):
    steps = []
    both = [d for r in range(1, depth) for d in (-r, r)]
    slices = range(SLICES)
    for k in slices:
        steps += [(name, k) for name in ("gs", "gf", "gu", "gd", "gp", "near")]
        steps += [("rows",)] if k == 0 else []
        steps += [("line", k, d) for d in both] + [("nline", k, d) for d in both]
        steps += [("pown", k)] + [("plane", k, d) for d in both] + [("side", k)]
        steps += [("tables",), ("scales",)] if k == 0 else []
        steps += [("expand", k, 0), ("expand", k, 1), ("middle", k), ("outer", k, 0), ("outer", k, 1)]
        steps += [("second", k, d, w) for d in range(depth) for w in (1, 0)]
    for k in slices:
        steps += [("lout", k, -d) for d in reversed(both)] + [("first", k, d) for d in range(depth)]
        steps += [("lsum", k), ("lfirst", k)] + [("zout", k, -d) for d in reversed(both)]
        steps += [("finish", k)]
    return steps + [("place", k) for k in slices]


ORDER = (
    ("gs", 0), ("gp", 0), ("rows",), ("gs", 1), ("gf", 0), ("gu", 0), ("gd", 1), ("gu", 1),
    ("gd", 0), ("gf", 1), ("near", 0), ("line", 0, -1), ("line", 0, 1), ("line", 0, -2),
    ("pown", 0), ("line", 0, -3), ("line", 0, 2), ("nline", 0, 1), ("nline", 0, 2),
    ("plane", 0, 1), ("nline", 0, -1), ("nline", 0, -2), ("gp", 1), ("nline", 0, -3),
    ("plane", 0, -1), ("line", 0, 3), ("near", 1), ("scales",), ("plane", 0, 2),
    ("line", 1, -1), ("nline", 0, 3), ("line", 1, 1), ("plane", 0, -2), ("nline", 1, 1),
    ("plane", 0, -3), ("side", 0), ("line", 1, 2), ("nline", 1, -1), ("plane", 0, 3),
    ("line", 1, -2), ("tables",), ("pown", 1), ("expand", 0, 0), ("line", 1, -3),
    ("line", 1, 3), ("expand", 0, 1), ("middle", 0), ("nline", 1, 3), ("nline", 1, -2),
    ("nline", 1, 2), ("plane", 1, 1), ("nline", 1, -3), ("plane", 1, -1), ("outer", 0, 0),
    ("outer", 0, 1), ("plane", 1, -2), ("plane", 1, 2), ("second", 0, 1, 1), ("lout", 0, 3),
    ("second", 0, 1, 0), ("second", 0, 3, 1), ("second", 0, 2, 0), ("lout", 0, -3),
    ("second", 0, 3, 0), ("plane", 1, -3), ("second", 0, 2, 1), ("plane", 1, 3),
    ("first", 0, 1), ("side", 1), ("lout", 0, 2), ("expand", 1, 0), ("lout", 0, -2),
    ("expand", 1, 1), ("middle", 1), ("first", 0, 3), ("zout", 0, -3), ("lout", 0, 1),
    ("outer", 1, 0), ("outer", 1, 1), ("lout", 1, 3), ("second", 1, 3, 1), ("second", 1, 1, 1),
    ("lout", 1, -3), ("first", 0, 2), ("lout", 0, -1), ("second", 1, 3, 0), ("lout", 1, 2),
    ("second", 1, 1, 0), ("second", 1, 2, 1), ("zout", 0, 3), ("first", 1, 3), ("zout", 0, -2),
    ("lout", 1, -2), ("zout", 0, 2), ("zout", 1, 3), ("first", 1, 1), ("second", 1, 2, 0),
    ("zout", 1, -3), ("lsum", 0), ("lout", 1, -1), ("lout", 1, 1), ("first", 1, 2),
    ("second", 0, 0, 1), ("second", 1, 0, 1), ("lfirst", 0), ("second", 0, 0, 0),
    ("zout", 1, -2), ("zout", 1, 2), ("first", 0, 0), ("zout", 0, -1), ("lsum", 1),
    ("zout", 0, 1), ("zout", 1, 1), ("second", 1, 0, 0), ("first", 1, 0), ("zout", 1, -1),
    ("lfirst", 1), ("finish", 0), ("place", 0), ("finish", 1), ("place", 1),
)


class Place:
    def __init__(self, devices):
        me = lax.axis_index("dp")
        self.depth = devices // 8
        self.me = me
        self.core = me % 2
        self.chip = me // 2
        x = self.chip % 2
        y = (self.chip // 2) % 2
        self.z = self.chip // 4
        dx = 1 - 2 * x
        dy = 2 * (1 - 2 * y)
        first = (1 - self.core) * dx + self.core * dy
        second = (1 - self.core) * dy + self.core * dx
        self.own = self.chip % 4
        self.near = self.own + first
        self.far = self.own + second
        self.diag = self.own + first + second
        self.sibling = me + 1 - 2 * self.core
        self.first = me + 2 * first
        self.second = me + 2 * second
        self.above = me + 8
        self.below = me - 8
        self.has_above = self.z + 1 < self.depth
        self.has_below = self.z >= 1

    def knock(self):
        barrier = pltpu.get_barrier_semaphore()

        def signal(peer):
            pl.semaphore_signal(
                barrier, inc=1, device_id={"dp": peer}, device_id_type=pl.DeviceIdType.MESH
            )

        for peer in (self.sibling, self.first, self.second):
            signal(peer)
        pl.when(self.has_above)(lambda: signal(self.above))
        pl.when(self.has_below)(lambda: signal(self.below))

        peers = 3 + self.has_above.astype(jnp.int32) + self.has_below.astype(jnp.int32)
        return lambda: pl.semaphore_wait(barrier, peers)


def remote(src, dst, send, recv, peer):
    return pltpu.make_async_remote_copy(
        src_ref=src,
        dst_ref=dst,
        send_sem=send,
        recv_sem=recv,
        device_id={"dp": peer},
        device_id_type=pl.DeviceIdType.MESH,
    )


class Layout:
    def __init__(self, devices, per, odd):
        self.split = per - odd
        self.depth = devices // 8
        self.sizes = (4 * (per - odd), 4 * odd)
        self.parts = (0, 1) if odd else (0,)
        self.plane = 16 * per
        self.total = self.depth * self.plane

    def part_of(self, j):
        return 0 if j < self.split else 1

    def first(self, part):
        return 0 if part == 0 else 2 * self.split

    def start(self, part, z, p):
        line, odd = self.sizes
        return z * self.plane + (p * line if part == 0 else 4 * line + p * odd)

    def piece(self, buf, k, part, z, p):
        span = pl.ds(self.start(part, z, p), self.sizes[part])
        return buf.at[span] if k is None else buf.at[k, span]

    def level(self, buf, k, z):
        line, odd = self.sizes
        span = pl.ds(z * self.plane + 4 * line, 4 * odd)
        return buf.at[span] if k is None else buf.at[k, span]


def fused_kernel(devices, pos_in, pos_out, own_in, own_out, tokens, cotangent, out,
                 full, stage, rows_h, rows_g, mats, grads, inverse,
                 tags, table, table_s, begin, begin_s, mid,
                 held, from_second, from_first, from_below, from_above, final, twin, flat,
                 load_sems, send_sems, pair_sems, twin_sems, tag_sems, gather_sems, level_sems,
                 second_sems, first_sems, below_sems, above_sems):
    at = Place(devices)
    depth = at.depth
    core = at.core
    per = own_in.shape[0]
    gat = [Layout(devices, per, odd) for odd in GATHER_PLANE]
    red = [Layout(devices, per, odd) for odd in REDUCE_PLANE]
    count, width = tokens.shape
    size = full[0].shape[1]
    half = BLOCK // 2
    rows_k = RANK // BLOCK
    rows_d = width // BLOCK
    blocks = rows_k * rows_d
    ranks = rows_k * size
    chunks = width // CHUNK
    sends = []
    waits = []

    def send(src, dst, recv, peer, present=None):
        remote(src, dst, send_sems.at[len(sends)], recv, peer).start()
        rows, whole = src.shape[0], src.dtype == jnp.int32
        if whole and len(src.shape) == 2:
            sends.append((lambda: tags.at[0], present))
        elif whole:
            sends.append((lambda: tags.at[pl.ds(0, rows)], present))
        else:
            sends.append((lambda: full[0].at[pl.ds(0, rows)], present))

    def got(buf, sem):
        remote(buf, buf, send_sems.at[0], sem, at.sibling).wait_recv()

    wait_peers = at.knock()

    own_rows = pl.ds(pl.multiple_of(core * count, count), count)
    local = [
        pltpu.make_async_copy(tokens, rows_h.at[own_rows], load_sems.at[0]),
        pltpu.make_async_copy(cotangent, rows_g.at[own_rows], load_sems.at[1]),
    ]
    for copy in local:
        copy.start()

    lanes = lax.broadcasted_iota(jnp.int32, tags.shape[1:], 1)
    row = jnp.full(tags.shape[1:], 2 * blocks, jnp.int32)
    for j in range(per):
        place = pos_in[0, j]
        row = jnp.where(lanes == 2 * j, jnp.where(place < blocks, place, 2 * blocks), row)
        row = jnp.where(lanes == 2 * j + 1, pos_out[0, j] + blocks, row)
    tags[at.me] = row

    for j in range(per):
        flat[0] = own_in[j].T
        flat[1] = own_out[j]
        for k in range(SLICES):
            lay = gat[k]
            part = lay.part_of(j)
            base = lay.start(part, at.z, at.own) + core * (lay.sizes[part] // 2)
            base += 2 * j - lay.first(part)
            keep = pl.ds(pl.multiple_of(core * half + k * size, size), size)
            give = pl.ds(pl.multiple_of((1 - core) * half + k * size, size), size)
            for m in range(2):
                full[k][base + m] = flat[m, keep, :]
                stage[k, 2 * j + m] = flat[m, give, :]
    for k in range(SLICES):
        full[k][gat[k].total] = jnp.zeros((size, BLOCK), jnp.bfloat16)
        grads[k][2 * blocks] = jnp.zeros((size, BLOCK), jnp.bfloat16)

    wait_peers()

    def pair(k, start):
        lay = gat[k]
        for part in lay.parts:
            n = lay.sizes[part] // 2
            base = lay.start(part, at.z, at.own) + core * n
            src, dst = stage.at[k, pl.ds(lay.first(part), n)], full[k].at[pl.ds(base, n)]
            if start:
                send(src, dst, pair_sems.at[k, part], at.sibling)
            else:
                got(src, pair_sems.at[k, part])

    send(tags.at[at.me], tags.at[at.me], tag_sems.at[2 * depth * 4], at.sibling)
    for k in range(SLICES):
        pair(k, True)

    def tag_piece(z, p):
        return tags.at[pl.ds(2 * (4 * z + p), 2)]

    def push(k, part, z, p, peer, present=None):
        if k == 0 and part == 0:
            piece = tag_piece(z, p)
            send(piece, piece, tag_sems.at[4 * z + p], peer, present)
        piece = gat[k].piece(full[k], None, part, z, p)
        send(piece, piece, gather_sems.at[k, part, 4 * z + p], peer, present)

    def arrived(k, part, z, p):
        if k == 0 and part == 0:
            got(tag_piece(z, p), tag_sems.at[4 * z + p])
        got(gat[k].piece(full[k], None, part, z, p), gather_sems.at[k, part, 4 * z + p])

    def inside(d):
        return (at.z + d < depth) if d > 0 else (at.z + d >= 0)

    def onward(d):
        return (at.has_below, at.below) if d > 0 else (at.has_above, at.above)

    def away(d):
        return (at.has_above, at.above) if d > 0 else (at.has_below, at.below)

    def own_second(k):
        pair(k, False)
        if k == 0:
            got(tags.at[at.me], tag_sems.at[2 * depth * 4])
        push(k, 0, at.z, at.own, at.second)

    def own_first(k):
        push(k, 0, at.z, at.own, at.first)

    def own_line(k, d):
        more, peer = away(d)
        pl.when(more)(lambda: push(k, 0, at.z, at.own, peer, lambda: more))

    def own_plane(k):
        for part in gat[k].parts[1:]:
            push(k, part, at.z, at.own, at.second)
            push(k, part, at.z, at.own, at.first)

    def near_own(k):
        for part in gat[k].parts:
            arrived(k, part, at.z, at.near)
            push(k, part, at.z, at.near, at.second)

    def line(k, d):
        more, peer = onward(d)
        here = inside(d)

        def run():
            z = at.z + d
            arrived(k, 0, z, at.own)
            pl.when(more)(lambda: push(k, 0, z, at.own, peer, lambda: more & here))
            push(k, 0, z, at.own, at.second, lambda: here)
            push(k, 0, z, at.own, at.first, lambda: here)

        pl.when(here)(run)

    def near_line(k, d):
        here = inside(d)

        def run():
            arrived(k, 0, at.z + d, at.near)
            push(k, 0, at.z + d, at.near, at.second, lambda: here)

        pl.when(here)(run)

    def push_level(k, z, peer, present):
        piece = gat[k].level(full[k], None, z)
        send(piece, piece, level_sems.at[k, z], peer, present)

    def plane_own(k):
        for part in gat[k].parts:
            for p in (at.far, at.diag):
                arrived(k, part, at.z, p)
        if gat[k].sizes[1]:
            for more, peer in (away(1), away(-1)):
                pl.when(more)(lambda more=more, peer=peer: push_level(k, at.z, peer, lambda: more))

    def plane(k, d):
        more, peer = onward(d)
        here = inside(d)

        def run():
            got(gat[k].level(full[k], None, at.z + d), level_sems.at[k, at.z + d])
            pl.when(more)(lambda: push_level(k, at.z + d, peer, lambda: more & here))

        if gat[k].sizes[1]:
            pl.when(here)(run)

    def side(k):
        for d in range(1 - depth, depth):

            def run(d=d):
                for p in (at.far, at.diag):
                    arrived(k, 0, at.z + d, p)

            if d:
                pl.when(inside(d))(run)

    def load_rows():
        swap = [
            remote(tokens, rows_h.at[own_rows], send_sems.at[len(sends)], load_sems.at[2], at.sibling),
            remote(cotangent, rows_g.at[own_rows], send_sems.at[len(sends) + 1], load_sems.at[3], at.sibling),
        ]
        for copy, src in zip(swap, (tokens, cotangent)):
            copy.start()
            sends.append((lambda src=src: src, None))
        waits.extend(swap)

    def scales():
        for copy in local:
            copy.wait()
        for copy in waits:
            copy.wait_recv()
        total = jnp.zeros((2 * count, BLOCK), jnp.float32)
        for i in range(0, width, BLOCK):
            wide = rows_h[:, i : i + BLOCK].astype(jnp.float32)
            total += wide * wide
        scale = jnp.sqrt(jnp.sum(total, axis=-1, keepdims=True) / width + EPS)
        inverse[...] = jnp.broadcast_to(1.0 / scale, inverse.shape)

    def tables():
        table[...] = tags[:, 0, :]
        copy = pltpu.make_async_copy(table, table_s, load_sems.at[4])
        copy.start()
        copy.wait()
        shape = begin[0].shape
        numbers = lax.broadcasted_iota(jnp.int32, shape, 0) * BLOCK
        numbers += lax.broadcasted_iota(jnp.int32, shape, 1)

        def scan(dev, found):
            z, p, which = dev // 8, (dev // 2) % 4, dev % 2
            found = list(found)
            for lane in range(2 * per):
                same = numbers == table_s[dev, lane]
                for k, lay in enumerate(gat):
                    part = lay.part_of(lane // 2)
                    entry = lay.start(part, z, p) + which * (lay.sizes[part] // 2)
                    found[k] = jnp.where(same, entry + lane - lay.first(part), found[k])
            return tuple(found)

        found = lax.fori_loop(
            0, devices, scan, tuple(jnp.full(shape, lay.total, jnp.int32) for lay in gat)
        )
        copies = []
        for k in range(SLICES):
            begin[k][...] = found[k]
            copies.append(pltpu.make_async_copy(begin[k], begin_s[k], load_sems.at[5 + k]))
            copies[k].start()
        for copy in copies:
            copy.wait()

    def expand(k, m):
        group = BLOCK // rows_k

        def step(low, carry, high):
            r = high * group + low
            into = pl.ds(pl.multiple_of(r * BLOCK, BLOCK), BLOCK)
            found = []
            for c in range(rows_k):
                if m == 0:
                    at_c = begin_s[k][high, low * rows_k + c]
                else:
                    b = blocks + c * rows_d + high * group
                    at_c = begin_s[k][b // BLOCK, b % BLOCK + low]
                found.append(full[k][at_c])
            for c in range(rows_k):
                mats[m, c * size : (c + 1) * size, into] = found[c]
            return carry

        for high in range(rows_d // group):
            lax.fori_loop(0, group, functools.partial(step, high=high), 0, unroll=4)

    def product(m):
        rows = rows_h if m == 0 else rows_g
        total = jnp.zeros((2 * count, ranks), jnp.float32)
        for i in range(0, width, CHUNK):
            total += lax.dot_general(
                rows[:, i : i + CHUNK], mats[m, :, i : i + CHUNK],
                (((1,), (1,)), ((), ())), preferred_element_type=jnp.float32,
            )
        return total

    def middle(k):
        scale = inverse[...] if ranks == BLOCK else inverse[:, :1]
        pre = product(0) * scale
        dact = product(1)
        sig = jax.nn.sigmoid(pre)
        dpre = dact * sig * (1.0 + pre * (1.0 - sig))
        mid[0] = (dpre * scale).T.astype(jnp.bfloat16)
        mid[1] = (pre * sig).T.astype(jnp.bfloat16)

    def outer(k, m):
        rows = rows_h if m == 0 else rows_g

        def step(i, carry):
            into = pl.ds(pl.multiple_of(i * CHUNK, CHUNK), CHUNK)
            part = lax.dot_general(
                mid[m], rows[:, into], (((1,), (0,)), ((), ())), preferred_element_type=jnp.float32
            ).astype(jnp.bfloat16)
            for r in range(CHUNK // BLOCK):
                col = i * (CHUNK // BLOCK) + r
                for c in range(rows_k):
                    b = col * rows_k + c if m == 0 else blocks + c * rows_d + col
                    grads[k][b] = part[c * size : (c + 1) * size, r * BLOCK : (r + 1) * BLOCK]
            return carry

        lax.fori_loop(0, chunks, step, 0)

    def fill(k, part, z, p, terms, into=None):
        lay = red[k]
        n = lay.sizes[part] // 2
        first = lay.first(part)
        base = lay.start(part, z, p)

        def step(which, carry):
            dev = 2 * (4 * z + p) + which
            for i in range(n):
                entry = base + which * n + i
                value = grads[k][table_s[dev, first + i]]
                if terms:
                    value = value.astype(jnp.float32)
                    for term in terms:
                        value += term[k, entry].astype(jnp.float32)
                    value = value.astype(jnp.bfloat16)
                if into is None:
                    held[k, entry] = value
                else:
                    into[k, 2 * first + which * n + i] = value
            return carry

        lax.fori_loop(0, 2, step, 0)

    def give(k, part, z, p, buf, sems, peer, present=None):
        src = red[k].piece(held, k, part, z, p)
        send(src, red[k].piece(buf, k, part, z, p), sems.at[k, part, 4 * z + p], peer, present)

    def take(k, part, z, p, buf, sems):
        got(red[k].piece(buf, k, part, z, p), sems.at[k, part, 4 * z + p])

    def behind(d):
        if d > 0:
            return at.has_below, from_below, below_sems, at.above
        return at.has_above, from_above, above_sems, at.below

    def level_out(k, d):
        before, buf, sems, peer = behind(d)
        here = inside(d)

        def run():
            z = at.z + d

            def fills(terms):
                for p in range(4):
                    fill(k, 1, z, p, terms)

            def summed():
                got(red[k].level(buf, k, z), sems.at[k, 1, z])
                fills([buf])

            pl.when(jnp.logical_not(before))(lambda: fills([]))
            pl.when(before)(summed)
            send(
                red[k].level(held, k, z), red[k].level(buf, k, z), sems.at[k, 1, z],
                peer, lambda: here,
            )

        if red[k].sizes[1]:
            pl.when(here)(run)

    def beside(run):
        above, below = at.has_above, at.has_below
        pl.when(below & above)(lambda: run([from_below, from_above]))
        pl.when(below & jnp.logical_not(above))(lambda: run([from_below]))
        pl.when(above & jnp.logical_not(below))(lambda: run([from_above]))

    def second(k, d, which):
        z = (at.z + d) % depth
        p = at.diag if which else at.far
        fill(k, 0, z, p, [])
        give(k, 0, z, p, from_second, second_sems, at.second)

    def first(k, d):
        z = (at.z + d) % depth
        take(k, 0, z, at.near, from_second, second_sems)
        fill(k, 0, z, at.near, [from_second])
        give(k, 0, z, at.near, from_first, first_sems, at.first)

    def level_sums(k):
        if not red[k].sizes[1]:
            return
        for more, buf, sems in (
            (at.has_below, from_below, below_sems), (at.has_above, from_above, above_sems)
        ):
            pl.when(more)(
                lambda buf=buf, sems=sems: got(red[k].level(buf, k, at.z), sems.at[k, 1, at.z])
            )

        def run(terms):
            for p in (at.diag, at.far):
                fill(k, 1, at.z, p, terms)

        beside(run)
        for p in (at.diag, at.far):
            give(k, 1, at.z, p, from_second, second_sems, at.second)

    def level_first(k):
        if not red[k].sizes[1]:
            return
        take(k, 1, at.z, at.near, from_second, second_sems)
        beside(lambda terms: fill(k, 1, at.z, at.near, [from_second] + terms))
        give(k, 1, at.z, at.near, from_first, first_sems, at.first)

    def line_out(k, d):
        before, buf, sems, peer = behind(d)
        here = inside(d)
        terms = [from_second, from_first]

        def run():
            z = at.z + d
            take(k, 0, z, at.own, from_second, second_sems)
            take(k, 0, z, at.own, from_first, first_sems)

            def summed():
                take(k, 0, z, at.own, buf, sems)
                fill(k, 0, z, at.own, terms + [buf])

            pl.when(jnp.logical_not(before))(lambda: fill(k, 0, z, at.own, terms))
            pl.when(before)(summed)
            give(k, 0, z, at.own, buf, sems, peer, lambda: here)

        pl.when(here)(run)

    def finish(k):
        lay = red[k]
        for part in lay.parts[::-1]:
            take(k, part, at.z, at.own, from_second, second_sems)
            take(k, part, at.z, at.own, from_first, first_sems)
        pl.when(at.has_below)(lambda: take(k, 0, at.z, at.own, from_below, below_sems))
        pl.when(at.has_above)(lambda: take(k, 0, at.z, at.own, from_above, above_sems))

        def run(terms):
            for part in lay.parts:
                fill(k, part, at.z, at.own, [from_second, from_first] + terms, final)

        beside(run)
        for part in lay.parts:
            n = lay.sizes[part] // 2
            piece = pl.ds(2 * lay.first(part) + (1 - core) * n, n)
            send(final.at[k, piece], twin.at[k, piece], twin_sems.at[k, part], at.sibling)

    def assemble(k):
        lay = red[k]
        for part in lay.parts:
            n = lay.sizes[part] // 2
            piece = pl.ds(2 * lay.first(part) + core * n, n)
            got(twin.at[k, piece], twin_sems.at[k, part])
        mine = pl.ds(pl.multiple_of(core * half + k * size, size), size)
        theirs = pl.ds(pl.multiple_of((1 - core) * half + k * size, size), size)
        for j in range(per):
            part = lay.part_of(j)
            entry = lay.first(part) + core * (lay.sizes[part] // 2) + 2 * j
            flat[j, mine, :] = final[k, entry]
            flat[j, theirs, :] = twin[k, entry]
            out[1, j, mine, :] = final[k, entry + 1]
            out[1, j, theirs, :] = twin[k, entry + 1]

    steps = {
        "gs": own_second, "gf": own_first, "gu": lambda k: own_line(k, 1),
        "gd": lambda k: own_line(k, -1), "gp": own_plane, "rows": load_rows,
        "near": near_own, "line": line, "nline": near_line, "pown": plane_own, "plane": plane,
        "side": side, "tables": tables, "scales": scales, "expand": expand, "middle": middle,
        "outer": outer, "lout": level_out, "second": second, "first": first,
        "lsum": level_sums, "lfirst": level_first, "zout": line_out, "finish": finish,
        "place": assemble,
    }
    for step in ORDER if depth == 4 and SLICES == 2 else plain_order(depth):
        steps[step[0]](*step[1:])
    for j in range(per):
        out[0, j] = flat[j].T
    for n, (like, present) in enumerate(sends):

        def sent(n=n, like=like):
            remote(like(), like(), send_sems.at[n], load_sems.at[0], at.sibling).wait_send()

        if present is None:
            sent()
        else:
            pl.when(present())(sent)


def one_section(tokens, blocks_in, blocks_out, pos_in, pos_out, cotangent):
    devices = lax.axis_size("dp")
    per = blocks_in.shape[1]
    count, width = tokens.shape
    depth = devices // 8
    chips = devices // 2
    entries = 4 * per * chips
    size = BLOCK // 2 // SLICES
    ranks = RANK // BLOCK * size
    blocks = (width // BLOCK) * (RANK // BLOCK)
    dma = pltpu.SemaphoreType.DMA
    vmem = pltpu.VMEM
    anywhere = pl.BlockSpec(memory_space=pl.ANY)
    scalars = pl.BlockSpec(memory_space=pltpu.SMEM)
    local = pl.BlockSpec(memory_space=vmem)
    bf16, f32, i32 = jnp.bfloat16, jnp.float32, jnp.int32
    shards = (SLICES, entries, size, BLOCK)
    words = -(-(2 * blocks + 1) // BLOCK)
    words = -(-words // 8) * 8
    results = pl.pallas_call(
        functools.partial(fused_kernel, devices),
        out_shape=jax.ShapeDtypeStruct((2, per, BLOCK, BLOCK), bf16),
        in_specs=[scalars, scalars, local, local, anywhere, anywhere],
        out_specs=local,
        scratch_shapes=[
            [vmem((entries + 1, size, BLOCK), bf16) for _ in range(SLICES)],
            vmem((SLICES, 2 * per, size, BLOCK), bf16),
            vmem((2 * count, width), bf16),
            vmem((2 * count, width), bf16),
            vmem((2, ranks, width), bf16),
            [vmem((2 * blocks + 1, size, BLOCK), bf16) for _ in range(SLICES)],
            vmem((2 * count, BLOCK), f32),
            vmem((devices, 8, BLOCK), i32),
            vmem((devices, BLOCK), i32),
            pltpu.SMEM((devices, BLOCK), i32),
            [vmem((words, BLOCK), i32) for _ in range(SLICES)],
            [pltpu.SMEM((words, BLOCK), i32) for _ in range(SLICES)],
            vmem((2, ranks, 2 * count), bf16),
            vmem(shards, bf16),
            vmem(shards, bf16),
            vmem(shards, bf16),
            vmem(shards, bf16),
            vmem(shards, bf16),
            vmem((SLICES, 4 * per, size, BLOCK), bf16),
            vmem((SLICES, 4 * per, size, BLOCK), bf16),
            vmem((per, BLOCK, BLOCK), bf16),
            dma((5 + SLICES,)),
            dma((400,)),
            dma((SLICES, 2)),
            dma((SLICES, 2)),
            dma((chips + 1 + chips,)),
            dma((SLICES, 2, chips)),
            dma((SLICES, depth)),
            dma((SLICES, 2, chips)),
            dma((SLICES, 2, chips)),
            dma((SLICES, 2, chips)),
            dma((SLICES, 2, chips)),
        ],
        compiler_params=pltpu.CompilerParams(
            collective_id=0, has_side_effects=True, vmem_limit_bytes=63 * 1024 * 1024
        ),
        name="fused_adapters",
    )(pos_in, pos_out, blocks_in[0], blocks_out[0], tokens, cotangent)
    return (results[0][None], results[1][None])


def solution(mesh):
    in_specs = (
        P("dp", None),
        P("section", "dp", None, None),
        P("section", "dp", None, None),
        P("section", "dp"),
        P("section", "dp"),
        P("dp", None),
    )
    out_specs = (P("section", "dp", None, None), P("section", "dp", None, None))
    body = one_section if mesh.shape["section"] == 1 else per_device
    return jax.shard_map(
        body, mesh=mesh, in_specs=in_specs, out_specs=out_specs, check_vma=False
    )
```

time: 139 us -> 103 us (0.74)
  Pallas kernels: 135 us -> 101 us
  local copies, waits for them, and re-layouts: 3.19 us -> 1.74 us
    pallas_call x1, Pallas kernels: 135 us -> 101 us  [one_section(): pl.pallas_call(functools.partial(fused_kernel, devices), out_shape=jax.Sh...]
    unnamed x2 -> x0, local copies, waits for them, and re-layouts: 3.19 us -> none
    slice x0 -> x1, local copies, waits for them, and re-layouts: none -> 1.74 us  [one_section(): return (results[0][None], results[1][None])]
where the time goes in v2:
time: 103 us
  Pallas kernels  101 us (98%)
  local copies, waits for them, and re-layouts  1.74 us (2%)
    pallas_call x1, Pallas kernels, one_section(): pl.pallas_call(functools.partial(fused_kernel, devices), out_shape=jax.Sh...  101 us

profile of v2, /device:TPU:1, one launch (start us, length us, event | category | flops | bytes accessed | tf_op | source)
XLA Modules:
  0.0 103.2 jit_solution(9863961457916148269)
XLA Ops:
  0.6 100.8 %fused_adapters.1 = bf16[2,5,128,128]{3,2,1,0:T(8,128)(2,1)} custom-call(s32[1,5]{1,0:T(1,128)} %pos_in.1, s32[1,5]{1,0:T(1,128)} %pos_out.1, bf16[5,128,128]{2,1,0:T(8,128)(2,1)} %bitcast.2, bf16[5,128,128]{2,1,0:T(8,128)(2,1)} %bitcast.3, bf16[128,8192]{1,0:T(8,128)(2,1)} %tokens.1, bf16[128,8192]{1,0:T(8,128)(2,1)} %cotangent.1), custom_call_target="tpu_custom_call" | custom-call | tf_op jit(solution)/shard_map/fused_adapters/pallas_call | solution.py:808
  101.5 1.7 %fusion = (bf16[1,5,128,128]{3,2,1,0:T(8,128)(2,1)}, bf16[1,5,128,128]{3,2,1,0:T(8,128)(2,1)}) fusion(bf16[2,5,128,128]{3,2,1,0:T(8,128)(2,1)} %fused_adapters.1), kind=kLoop, calls=%fused_computation | loop fusion | bytes 655360 | tf_op jit(solution)/shard_map/slice | solution.py:852

commit v3 on v2

--- a/solution.py
+++ b/solution.py
@@ -194,30 +194,29 @@
 
 
 ORDER = (
-    ("gs", 0), ("gp", 0), ("rows",), ("gs", 1), ("gf", 0), ("gu", 0), ("gd", 1), ("gu", 1),
-    ("gd", 0), ("gf", 1), ("near", 0), ("line", 0, -1), ("line", 0, 1), ("line", 0, -2),
-    ("pown", 0), ("line", 0, -3), ("line", 0, 2), ("nline", 0, 1), ("nline", 0, 2),
-    ("plane", 0, 1), ("nline", 0, -1), ("nline", 0, -2), ("gp", 1), ("nline", 0, -3),
-    ("plane", 0, -1), ("line", 0, 3), ("near", 1), ("scales",), ("plane", 0, 2),
-    ("line", 1, -1), ("nline", 0, 3), ("line", 1, 1), ("plane", 0, -2), ("nline", 1, 1),
-    ("plane", 0, -3), ("side", 0), ("line", 1, 2), ("nline", 1, -1), ("plane", 0, 3),
-    ("line", 1, -2), ("tables",), ("pown", 1), ("expand", 0, 0), ("line", 1, -3),
-    ("line", 1, 3), ("expand", 0, 1), ("middle", 0), ("nline", 1, 3), ("nline", 1, -2),
-    ("nline", 1, 2), ("plane", 1, 1), ("nline", 1, -3), ("plane", 1, -1), ("outer", 0, 0),
-    ("outer", 0, 1), ("plane", 1, -2), ("plane", 1, 2), ("second", 0, 1, 1), ("lout", 0, 3),
-    ("second", 0, 1, 0), ("second", 0, 3, 1), ("second", 0, 2, 0), ("lout", 0, -3),
-    ("second", 0, 3, 0), ("plane", 1, -3), ("second", 0, 2, 1), ("plane", 1, 3),
-    ("first", 0, 1), ("side", 1), ("lout", 0, 2), ("expand", 1, 0), ("lout", 0, -2),
-    ("expand", 1, 1), ("middle", 1), ("first", 0, 3), ("zout", 0, -3), ("lout", 0, 1),
-    ("outer", 1, 0), ("outer", 1, 1), ("lout", 1, 3), ("second", 1, 3, 1), ("second", 1, 1, 1),
-    ("lout", 1, -3), ("first", 0, 2), ("lout", 0, -1), ("second", 1, 3, 0), ("lout", 1, 2),
-    ("second", 1, 1, 0), ("second", 1, 2, 1), ("zout", 0, 3), ("first", 1, 3), ("zout", 0, -2),
-    ("lout", 1, -2), ("zout", 0, 2), ("zout", 1, 3), ("first", 1, 1), ("second", 1, 2, 0),
-    ("zout", 1, -3), ("lsum", 0), ("lout", 1, -1), ("lout", 1, 1), ("first", 1, 2),
-    ("second", 0, 0, 1), ("second", 1, 0, 1), ("lfirst", 0), ("second", 0, 0, 0),
-    ("zout", 1, -2), ("zout", 1, 2), ("first", 0, 0), ("zout", 0, -1), ("lsum", 1),
-    ("zout", 0, 1), ("zout", 1, 1), ("second", 1, 0, 0), ("first", 1, 0), ("zout", 1, -1),
-    ("lfirst", 1), ("finish", 0), ("place", 0), ("finish", 1), ("place", 1),
+    ("gs", 0), ("gu", 0), ("gf", 0), ("gp", 0), ("rows",), ("gs", 1), ("gd", 0), ("near", 0),
+    ("line", 0, 1), ("gd", 1), ("line", 0, -1), ("line", 0, -2), ("line", 0, 2), ("pown", 0),
+    ("gf", 1), ("nline", 0, 1), ("line", 0, -3), ("nline", 0, -1), ("nline", 0, -3),
+    ("line", 0, 3), ("nline", 0, 2), ("plane", 0, 1), ("plane", 0, -1), ("gu", 1), ("scales",),
+    ("nline", 0, 3), ("plane", 0, 2), ("plane", 0, -2), ("nline", 0, -2), ("gp", 1),
+    ("near", 1), ("line", 1, -1), ("plane", 0, 3), ("plane", 0, -3), ("line", 1, 1),
+    ("side", 0), ("tables",), ("line", 1, -2), ("line", 1, 2), ("expand", 0, 0), ("pown", 1),
+    ("expand", 0, 1), ("nline", 1, 1), ("nline", 1, -1), ("line", 1, -3), ("line", 1, 3),
+    ("middle", 0), ("plane", 1, -1), ("plane", 1, 1), ("nline", 1, 2), ("nline", 1, -2),
+    ("outer", 0, 0), ("nline", 1, 3), ("nline", 1, -3), ("plane", 1, -2), ("outer", 0, 1),
+    ("plane", 1, 2), ("second", 0, 3, 1), ("lout", 0, 3), ("lout", 0, -3), ("second", 0, 2, 1),
+    ("second", 0, 1, 1), ("side", 1), ("second", 0, 3, 0), ("second", 0, 1, 0),
+    ("second", 0, 2, 0), ("plane", 1, 3), ("plane", 1, -3), ("expand", 1, 0), ("lout", 0, 2),
+    ("expand", 1, 1), ("lout", 0, -2), ("first", 0, 3), ("middle", 1), ("first", 0, 2),
+    ("lout", 0, 1), ("first", 0, 1), ("lout", 0, -1), ("outer", 1, 0), ("zout", 0, 3),
+    ("outer", 1, 1), ("second", 1, 3, 1), ("lout", 1, 3), ("second", 1, 1, 1), ("zout", 0, 2),
+    ("lout", 1, -3), ("second", 1, 2, 1), ("zout", 0, -3), ("lout", 1, -2), ("first", 1, 3),
+    ("second", 1, 1, 0), ("second", 1, 3, 0), ("second", 1, 2, 0), ("first", 1, 1), ("lsum", 0),
+    ("lout", 1, 2), ("lout", 1, -1), ("second", 1, 0, 1), ("second", 0, 0, 1), ("lout", 1, 1),
+    ("zout", 1, -3), ("zout", 1, 3), ("zout", 0, 1), ("zout", 0, -2), ("first", 1, 2),
+    ("lsum", 1), ("zout", 1, -2), ("lfirst", 0), ("second", 0, 0, 0), ("zout", 1, 2),
+    ("first", 1, 0), ("zout", 0, -1), ("second", 1, 0, 0), ("first", 0, 0), ("zout", 1, -1),
+    ("zout", 1, 1), ("lfirst", 1), ("finish", 0), ("finish", 1), ("place", 0), ("place", 1),
 )
 
 
@@ -304,8 +303,8 @@
         return buf.at[span] if k is None else buf.at[k, span]
 
 
-def fused_kernel(devices, pos_in, pos_out, own_in, own_out, tokens, cotangent, out,
-                 full, stage, rows_h, rows_g, mats, grads, inverse,
+def fused_kernel(devices, pos_in, pos_out, blocks_in, blocks_out, tokens, cotangent, out,
+                 own, full, stage, rows_h, rows_g, mats, grads, inverse,
                  tags, table, table_s, begin, begin_s, mid,
                  held, from_second, from_first, from_below, from_above, final, twin, flat,
                  load_sems, send_sems, pair_sems, twin_sems, tag_sems, gather_sems, level_sems,
@@ -313,7 +312,7 @@
     at = Place(devices)
     depth = at.depth
     core = at.core
-    per = own_in.shape[0]
+    per = blocks_in.shape[0]
     gat = [Layout(devices, per, odd) for odd in GATHER_PLANE]
     red = [Layout(devices, per, odd) for odd in REDUCE_PLANE]
     count, width = tokens.shape
@@ -341,6 +340,12 @@
         remote(buf, buf, send_sems.at[0], sem, at.sibling).wait_recv()
 
     wait_peers = at.knock()
+    own_loads = [
+        pltpu.make_async_copy(blocks_in, own.at[0], load_sems.at[5]),
+        pltpu.make_async_copy(blocks_out, own.at[1], load_sems.at[6]),
+    ]
+    for copy in own_loads:
+        copy.start()
 
     own_rows = pl.ds(pl.multiple_of(core * count, count), count)
     local = [
@@ -358,9 +363,11 @@
         row = jnp.where(lanes == 2 * j + 1, pos_out[0, j] + blocks, row)
     tags[at.me] = row
 
+    for copy in own_loads:
+        copy.wait()
     for j in range(per):
-        flat[0] = own_in[j].T
-        flat[1] = own_out[j]
+        flat[0] = own[0, j].T
+        flat[1] = own[1, j]
         for k in range(SLICES):
             lay = gat[k]
             part = lay.part_of(j)
@@ -388,7 +395,7 @@
             else:
                 got(src, pair_sems.at[k, part])
 
-    send(tags.at[at.me], tags.at[at.me], tag_sems.at[2 * depth * 4], at.sibling)
+    send(tags.at[at.me], tags.at[at.me], tag_sems.at[4 * depth], at.sibling)
     for k in range(SLICES):
         pair(k, True)
 
@@ -400,12 +407,12 @@
             piece = tag_piece(z, p)
             send(piece, piece, tag_sems.at[4 * z + p], peer, present)
         piece = gat[k].piece(full[k], None, part, z, p)
-        send(piece, piece, gather_sems.at[k, part, 4 * z + p], peer, present)
+        send(piece, piece, gather_sems.at[k, 4 * z + p if part == 0 else 4 * depth + p], peer, present)
 
     def arrived(k, part, z, p):
         if k == 0 and part == 0:
             got(tag_piece(z, p), tag_sems.at[4 * z + p])
-        got(gat[k].piece(full[k], None, part, z, p), gather_sems.at[k, part, 4 * z + p])
+        got(gat[k].piece(full[k], None, part, z, p), gather_sems.at[k, 4 * z + p if part == 0 else 4 * depth + p])
 
     def inside(d):
         return (at.z + d < depth) if d > 0 else (at.z + d >= 0)
@@ -419,7 +426,7 @@
     def own_second(k):
         pair(k, False)
         if k == 0:
-            got(tags.at[at.me], tag_sems.at[2 * depth * 4])
+            got(tags.at[at.me], tag_sems.at[4 * depth])
         push(k, 0, at.z, at.own, at.second)
 
     def own_first(k):
@@ -525,24 +532,32 @@
         numbers = lax.broadcasted_iota(jnp.int32, shape, 0) * BLOCK
         numbers += lax.broadcasted_iota(jnp.int32, shape, 1)
 
+        kinds = {lay.split: lay for lay in gat}
+
         def scan(dev, found):
             z, p, which = dev // 8, (dev // 2) % 4, dev % 2
+            bases = [
+                [lay.start(part, z, p) + which * (lay.sizes[part] // 2) for part in range(2)]
+                for lay in kinds.values()
+            ]
             found = list(found)
             for lane in range(2 * per):
                 same = numbers == table_s[dev, lane]
-                for k, lay in enumerate(gat):
+                for n, lay in enumerate(kinds.values()):
                     part = lay.part_of(lane // 2)
-                    entry = lay.start(part, z, p) + which * (lay.sizes[part] // 2)
-                    found[k] = jnp.where(same, entry + lane - lay.first(part), found[k])
+                    entry = bases[n][part] + (lane - lay.first(part))
+                    found[n] = jnp.where(same, entry, found[n])
             return tuple(found)
 
         found = lax.fori_loop(
-            0, devices, scan, tuple(jnp.full(shape, lay.total, jnp.int32) for lay in gat)
+            0, devices, scan,
+            tuple(jnp.full(shape, lay.total, jnp.int32) for lay in kinds.values()),
         )
+        found = dict(zip(kinds, found))
         copies = []
         for k in range(SLICES):
-            begin[k][...] = found[k]
-            copies.append(pltpu.make_async_copy(begin[k], begin_s[k], load_sems.at[5 + k]))
+            begin[k][...] = found[gat[k].split]
+            copies.append(pltpu.make_async_copy(begin[k], begin_s[k], load_sems.at[7 + k]))
             copies[k].start()
         for copy in copies:
             copy.wait()
@@ -579,7 +594,7 @@
         return total
 
     def middle(k):
-        scale = inverse[...] if ranks == BLOCK else inverse[:, :1]
+        scale = inverse[:, :ranks] if ranks <= BLOCK else inverse[:, :1]
         pre = product(0) * scale
         dact = product(1)
         sig = jax.nn.sigmoid(pre)
@@ -628,12 +643,18 @@
 
         lax.fori_loop(0, 2, step, 0)
 
-    def give(k, part, z, p, buf, sems, peer, present=None):
+    def give(k, part, z, p, buf, sem, peer, present=None):
         src = red[k].piece(held, k, part, z, p)
-        send(src, red[k].piece(buf, k, part, z, p), sems.at[k, part, 4 * z + p], peer, present)
-
-    def take(k, part, z, p, buf, sems):
-        got(red[k].piece(buf, k, part, z, p), sems.at[k, part, 4 * z + p])
+        send(src, red[k].piece(buf, k, part, z, p), sem, peer, present)
+
+    def take(k, part, z, p, buf, sem):
+        got(red[k].piece(buf, k, part, z, p), sem)
+
+    def sem_second(k, part, z, passed):
+        return second_sems.at[k, passed, z if part == 0 else depth]
+
+    def sem_first(k, part, z):
+        return first_sems.at[k, z if part == 0 else depth]
 
     def behind(d):
         if d > 0:
@@ -675,13 +696,13 @@
         z = (at.z + d) % depth
         p = at.diag if which else at.far
         fill(k, 0, z, p, [])
-        give(k, 0, z, p, from_second, second_sems, at.second)
+        give(k, 0, z, p, from_second, sem_second(k, 0, z, which), at.second)
 
     def first(k, d):
         z = (at.z + d) % depth
-        take(k, 0, z, at.near, from_second, second_sems)
+        take(k, 0, z, at.near, from_second, sem_second(k, 0, z, 1))
         fill(k, 0, z, at.near, [from_second])
-        give(k, 0, z, at.near, from_first, first_sems, at.first)
+        give(k, 0, z, at.near, from_first, sem_first(k, 0, z), at.first)
 
     def level_sums(k):
         if not red[k].sizes[1]:
@@ -698,15 +719,15 @@
                 fill(k, 1, at.z, p, terms)
 
         beside(run)
-        for p in (at.diag, at.far):
-            give(k, 1, at.z, p, from_second, second_sems, at.second)
+        for passed, p in ((1, at.diag), (0, at.far)):
+            give(k, 1, at.z, p, from_second, sem_second(k, 1, at.z, passed), at.second)
 
     def level_first(k):
         if not red[k].sizes[1]:
             return
-        take(k, 1, at.z, at.near, from_second, second_sems)
+        take(k, 1, at.z, at.near, from_second, sem_second(k, 1, at.z, 1))
         beside(lambda terms: fill(k, 1, at.z, at.near, [from_second] + terms))
-        give(k, 1, at.z, at.near, from_first, first_sems, at.first)
+        give(k, 1, at.z, at.near, from_first, sem_first(k, 1, at.z), at.first)
 
     def line_out(k, d):
         before, buf, sems, peer = behind(d)
@@ -715,26 +736,26 @@
 
         def run():
             z = at.z + d
-            take(k, 0, z, at.own, from_second, second_sems)
-            take(k, 0, z, at.own, from_first, first_sems)
+            take(k, 0, z, at.own, from_second, sem_second(k, 0, z, 0))
+            take(k, 0, z, at.own, from_first, sem_first(k, 0, z))
 
             def summed():
-                take(k, 0, z, at.own, buf, sems)
+                take(k, 0, z, at.own, buf, sems.at[k, 0, z])
                 fill(k, 0, z, at.own, terms + [buf])
 
             pl.when(jnp.logical_not(before))(lambda: fill(k, 0, z, at.own, terms))
             pl.when(before)(summed)
-            give(k, 0, z, at.own, buf, sems, peer, lambda: here)
+            give(k, 0, z, at.own, buf, sems.at[k, 0, z], peer, lambda: here)
 
         pl.when(here)(run)
 
     def finish(k):
         lay = red[k]
         for part in lay.parts[::-1]:
-            take(k, part, at.z, at.own, from_second, second_sems)
-            take(k, part, at.z, at.own, from_first, first_sems)
-        pl.when(at.has_below)(lambda: take(k, 0, at.z, at.own, from_below, below_sems))
-        pl.when(at.has_above)(lambda: take(k, 0, at.z, at.own, from_above, above_sems))
+            take(k, part, at.z, at.own, from_second, sem_second(k, part, at.z, 0))
+            take(k, part, at.z, at.own, from_first, sem_first(k, part, at.z))
+        pl.when(at.has_below)(lambda: take(k, 0, at.z, at.own, from_below, below_sems.at[k, 0, at.z]))
+        pl.when(at.has_above)(lambda: take(k, 0, at.z, at.own, from_above, above_sems.at[k, 0, at.z]))
 
         def run(terms):
             for part in lay.parts:
@@ -771,7 +792,7 @@
         "lsum": level_sums, "lfirst": level_first, "zout": line_out, "finish": finish,
         "place": assemble,
     }
-    for step in ORDER if depth == 4 and SLICES == 2 else plain_order(depth):
+    for step in ORDER if depth == 4 else plain_order(depth):
         steps[step[0]](*step[1:])
     for j in range(per):
         out[0, j] = flat[j].T
@@ -793,6 +814,7 @@
     depth = devices // 8
     chips = devices // 2
     entries = 4 * per * chips
+    sends = 8 * depth + SLICES * (15 + 14 * depth)
     size = BLOCK // 2 // SLICES
     ranks = RANK // BLOCK * size
     blocks = (width // BLOCK) * (RANK // BLOCK)
@@ -808,9 +830,10 @@
     results = pl.pallas_call(
         functools.partial(fused_kernel, devices),
         out_shape=jax.ShapeDtypeStruct((2, per, BLOCK, BLOCK), bf16),
-        in_specs=[scalars, scalars, local, local, anywhere, anywhere],
+        in_specs=[scalars, scalars] + [anywhere] * 4,
         out_specs=local,
         scratch_shapes=[
+            vmem((2, per, BLOCK, BLOCK), bf16),
             [vmem((entries + 1, size, BLOCK), bf16) for _ in range(SLICES)],
             vmem((SLICES, 2 * per, size, BLOCK), bf16),
             vmem((2 * count, width), bf16),
@@ -832,17 +855,17 @@
             vmem((SLICES, 4 * per, size, BLOCK), bf16),
             vmem((SLICES, 4 * per, size, BLOCK), bf16),
             vmem((per, BLOCK, BLOCK), bf16),
-            dma((5 + SLICES,)),
-            dma((400,)),
+            dma((7 + SLICES,)),
+            dma((sends,)),
             dma((SLICES, 2)),
             dma((SLICES, 2)),
-            dma((chips + 1 + chips,)),
-            dma((SLICES, 2, chips)),
+            dma((chips + 1,)),
+            dma((SLICES, chips + 4)),
             dma((SLICES, depth)),
-            dma((SLICES, 2, chips)),
-            dma((SLICES, 2, chips)),
-            dma((SLICES, 2, chips)),
-            dma((SLICES, 2, chips)),
+            dma((SLICES, 2, depth + 1)),
+            dma((SLICES, depth + 1)),
+            dma((SLICES, 2, depth)),
+            dma((SLICES, 2, depth)),
         ],
         compiler_params=pltpu.CompilerParams(
             collective_id=0, has_side_effects=True, vmem_limit_bytes=63 * 1024 * 1024

time: 103 us -> 96.3 us (0.935)
  Pallas kernels: 101 us -> 93.7 us
    pallas_call x1, Pallas kernels: 101 us -> 93.7 us  [one_section(): pl.pallas_call(functools.partial(fused_kernel, devices), out_shape=jax.Sh...]
where the time goes in v3:
time: 96.3 us; the launch traced here: 96.1 us
  Pallas kernels  93.7 us (97%)
  local copies, waits for them, and re-layouts  1.74 us (2%)
    pallas_call x1, Pallas kernels, one_section(): pl.pallas_call(functools.partial(fused_kernel, devices), out_shape=jax.Sh...  93.7 us

profile of v3, /device:TPU:1, one launch (start us, length us, event | category | flops | bytes accessed | tf_op | source)
XLA Modules:
  0.0 96.1 jit_solution(5781399856830261460)
XLA Ops:
  0.6 93.7 %fused_adapters.1 = bf16[2,5,128,128]{3,2,1,0:T(8,128)(2,1)} custom-call(s32[1,5]{1,0:T(1,128)} %pos_in.1, s32[1,5]{1,0:T(1,128)} %pos_out.1, bf16[5,128,128]{2,1,0:T(8,128)(2,1)} %bitcast.2, bf16[5,128,128]{2,1,0:T(8,128)(2,1)} %bitcast.3, bf16[128,8192]{1,0:T(8,128)(2,1)} %tokens.1, bf16[128,8192]{1,0:T(8,128)(2,1)} %cotangent.1), custom_call_target="tpu_custom_call" | custom-call | tf_op jit(solution)/shard_map/fused_adapters/pallas_call | solution.py:830
  94.4 1.7 %fusion = (bf16[1,5,128,128]{3,2,1,0:T(8,128)(2,1)}, bf16[1,5,128,128]{3,2,1,0:T(8,128)(2,1)}) fusion(bf16[2,5,128,128]{3,2,1,0:T(8,128)(2,1)} %fused_adapters.1), kind=kLoop, calls=%fused_computation | loop fusion | bytes 655360 | tf_op jit(solution)/shard_map/slice | solution.py:875

commit v4 on v3

--- a/solution.py
+++ b/solution.py
@@ -194,29 +194,30 @@
 
 
 ORDER = (
-    ("gs", 0), ("gu", 0), ("gf", 0), ("gp", 0), ("rows",), ("gs", 1), ("gd", 0), ("near", 0),
-    ("line", 0, 1), ("gd", 1), ("line", 0, -1), ("line", 0, -2), ("line", 0, 2), ("pown", 0),
-    ("gf", 1), ("nline", 0, 1), ("line", 0, -3), ("nline", 0, -1), ("nline", 0, -3),
-    ("line", 0, 3), ("nline", 0, 2), ("plane", 0, 1), ("plane", 0, -1), ("gu", 1), ("scales",),
-    ("nline", 0, 3), ("plane", 0, 2), ("plane", 0, -2), ("nline", 0, -2), ("gp", 1),
-    ("near", 1), ("line", 1, -1), ("plane", 0, 3), ("plane", 0, -3), ("line", 1, 1),
-    ("side", 0), ("tables",), ("line", 1, -2), ("line", 1, 2), ("expand", 0, 0), ("pown", 1),
-    ("expand", 0, 1), ("nline", 1, 1), ("nline", 1, -1), ("line", 1, -3), ("line", 1, 3),
-    ("middle", 0), ("plane", 1, -1), ("plane", 1, 1), ("nline", 1, 2), ("nline", 1, -2),
-    ("outer", 0, 0), ("nline", 1, 3), ("nline", 1, -3), ("plane", 1, -2), ("outer", 0, 1),
-    ("plane", 1, 2), ("second", 0, 3, 1), ("lout", 0, 3), ("lout", 0, -3), ("second", 0, 2, 1),
-    ("second", 0, 1, 1), ("side", 1), ("second", 0, 3, 0), ("second", 0, 1, 0),
-    ("second", 0, 2, 0), ("plane", 1, 3), ("plane", 1, -3), ("expand", 1, 0), ("lout", 0, 2),
-    ("expand", 1, 1), ("lout", 0, -2), ("first", 0, 3), ("middle", 1), ("first", 0, 2),
-    ("lout", 0, 1), ("first", 0, 1), ("lout", 0, -1), ("outer", 1, 0), ("zout", 0, 3),
-    ("outer", 1, 1), ("second", 1, 3, 1), ("lout", 1, 3), ("second", 1, 1, 1), ("zout", 0, 2),
-    ("lout", 1, -3), ("second", 1, 2, 1), ("zout", 0, -3), ("lout", 1, -2), ("first", 1, 3),
-    ("second", 1, 1, 0), ("second", 1, 3, 0), ("second", 1, 2, 0), ("first", 1, 1), ("lsum", 0),
-    ("lout", 1, 2), ("lout", 1, -1), ("second", 1, 0, 1), ("second", 0, 0, 1), ("lout", 1, 1),
-    ("zout", 1, -3), ("zout", 1, 3), ("zout", 0, 1), ("zout", 0, -2), ("first", 1, 2),
-    ("lsum", 1), ("zout", 1, -2), ("lfirst", 0), ("second", 0, 0, 0), ("zout", 1, 2),
-    ("first", 1, 0), ("zout", 0, -1), ("second", 1, 0, 0), ("first", 0, 0), ("zout", 1, -1),
-    ("zout", 1, 1), ("lfirst", 1), ("finish", 0), ("finish", 1), ("place", 0), ("place", 1),
+    ("gs", 0), ("gd", 0), ("gs", 1), ("gf", 0), ("gp", 0), ("rows",), ("gu", 0), ("near", 0),
+    ("line", 0, 1), ("line", 0, -1), ("gf", 1), ("gu", 1), ("line", 0, -2), ("line", 0, 2),
+    ("pown", 0), ("scales",), ("nline", 0, -1), ("line", 0, -3), ("nline", 0, 1),
+    ("plane", 0, -1), ("line", 0, 3), ("plane", 0, 1), ("nline", 0, -2), ("nline", 0, 3),
+    ("gd", 1), ("nline", 0, -3), ("plane", 0, -2), ("nline", 0, 2), ("plane", 0, 2), ("gp", 1),
+    ("near", 1), ("line", 1, 1), ("plane", 0, -3), ("line", 1, -1), ("plane", 0, 3),
+    ("side", 0), ("tables",), ("line", 1, 2), ("line", 1, -2), ("expand", 0, 0),
+    ("nline", 1, 1), ("pown", 1), ("expand", 0, 1), ("nline", 1, -1), ("line", 1, 3),
+    ("middle", 0), ("nline", 1, -2), ("plane", 1, 1), ("nline", 1, 2), ("line", 1, -3),
+    ("plane", 1, -1), ("outer", 0, 0), ("nline", 1, -3), ("nline", 1, 3), ("outer", 0, 1),
+    ("plane", 1, -2), ("plane", 1, 2), ("second", 0, 3, 1), ("lout", 0, -3), ("lout", 0, 3),
+    ("second", 0, 1, 1), ("second", 0, 2, 1), ("side", 1), ("second", 0, 3, 0),
+    ("second", 0, 1, 0), ("second", 0, 2, 0), ("plane", 1, 3), ("plane", 1, -3),
+    ("expand", 1, 0), ("first", 0, 3), ("lout", 0, -2), ("lout", 0, 2), ("expand", 1, 1),
+    ("first", 0, 1), ("middle", 1), ("lout", 0, -1), ("lout", 0, 1), ("first", 0, 2),
+    ("outer", 1, 0), ("zout", 0, 3), ("outer", 1, 1), ("lout", 1, -3), ("second", 1, 3, 1),
+    ("second", 1, 1, 1), ("second", 1, 2, 1), ("lout", 1, 3), ("second", 1, 1, 0),
+    ("second", 1, 3, 0), ("zout", 0, -3), ("second", 1, 2, 0), ("lout", 1, -2), ("first", 1, 3),
+    ("lout", 1, 2), ("first", 1, 1), ("second", 1, 0, 1), ("lout", 1, -1), ("zout", 1, -3),
+    ("lout", 1, 1), ("zout", 0, 2), ("lsum", 0), ("zout", 1, 3), ("first", 1, 2),
+    ("second", 0, 0, 1), ("zout", 0, -2), ("zout", 1, -2), ("zout", 0, 1), ("first", 1, 0),
+    ("second", 0, 0, 0), ("lsum", 1), ("zout", 0, -1), ("zout", 1, 2), ("first", 0, 0),
+    ("second", 1, 0, 0), ("zout", 1, -1), ("zout", 1, 1), ("lfirst", 0), ("lfirst", 1),
+    ("finish", 0), ("finish", 1), ("place", 0), ("place", 1),
 )
 
 
@@ -307,7 +308,7 @@
                  own, full, stage, rows_h, rows_g, mats, grads, inverse,
                  tags, table, table_s, begin, begin_s, mid,
                  held, from_second, from_first, from_below, from_above, final, twin, flat,
-                 load_sems, send_sems, pair_sems, twin_sems, tag_sems, gather_sems, level_sems,
+                 load_sems, send_sems, group_sems, pair_sems, twin_sems, tag_sems, gather_sems, level_sems,
                  second_sems, first_sems, below_sems, above_sems):
     at = Place(devices)
     depth = at.depth
@@ -325,16 +326,33 @@
     chunks = width // CHUNK
     sends = []
     waits = []
-
-    def send(src, dst, recv, peer, present=None):
-        remote(src, dst, send_sems.at[len(sends)], recv, peer).start()
-        rows, whole = src.shape[0], src.dtype == jnp.int32
-        if whole and len(src.shape) == 2:
-            sends.append((lambda: tags.at[0], present))
-        elif whole:
-            sends.append((lambda: tags.at[pl.ds(0, rows)], present))
+    groups = {}
+    singles = []
+
+    def groups_at(name):
+        return group_sems.at[groups[name]]
+
+
+    def like(kind, rows):
+        if kind == "tag":
+            return tags.at[0]
+        return tags.at[pl.ds(0, rows)] if kind == "tags" else full[0].at[pl.ds(0, rows)]
+
+    def send(src, dst, recv, peer, present=None, group=None):
+        whole = src.dtype == jnp.int32
+        kind = ("tag" if len(src.shape) == 2 else "tags") if whole else "blocks"
+        if group is not None:
+            name, copies = group
+            name += (kind,)
+            if name not in groups:
+                groups[name] = len(groups)
+                sends.append((True, groups[name], kind, copies * src.shape[0], None))
+            sem = groups_at(name)
         else:
-            sends.append((lambda: full[0].at[pl.ds(0, rows)], present))
+            singles.append(present)
+            sem = send_sems.at[len(singles) - 1]
+            sends.append((False, len(singles) - 1, kind, src.shape[0], present))
+        remote(src, dst, sem, recv, peer).start()
 
     def got(buf, sem):
         remote(buf, buf, send_sems.at[0], sem, at.sibling).wait_recv()
@@ -403,11 +421,16 @@
         return tags.at[pl.ds(2 * (4 * z + p), 2)]
 
     def push(k, part, z, p, peer, present=None):
+        group = None
+        if peer is at.second:
+            group = (("gather", k, part, 2), 2 * depth if part == 0 else 2)
+        elif peer is at.first:
+            group = (("gather", k, part, 1), depth if part == 0 else 1)
         if k == 0 and part == 0:
             piece = tag_piece(z, p)
-            send(piece, piece, tag_sems.at[4 * z + p], peer, present)
+            send(piece, piece, tag_sems.at[4 * z + p], peer, present, group)
         piece = gat[k].piece(full[k], None, part, z, p)
-        send(piece, piece, gather_sems.at[k, 4 * z + p if part == 0 else 4 * depth + p], peer, present)
+        send(piece, piece, gather_sems.at[k, 4 * z + p if part == 0 else 4 * depth + p], peer, present, group)
 
     def arrived(k, part, z, p):
         if k == 0 and part == 0:
@@ -503,12 +526,11 @@
 
     def load_rows():
         swap = [
-            remote(tokens, rows_h.at[own_rows], send_sems.at[len(sends)], load_sems.at[2], at.sibling),
-            remote(cotangent, rows_g.at[own_rows], send_sems.at[len(sends) + 1], load_sems.at[3], at.sibling),
+            remote(tokens, rows_h.at[own_rows], load_sems.at[7 + SLICES], load_sems.at[2], at.sibling),
+            remote(cotangent, rows_g.at[own_rows], load_sems.at[8 + SLICES], load_sems.at[3], at.sibling),
         ]
-        for copy, src in zip(swap, (tokens, cotangent)):
+        for copy in swap:
             copy.start()
-            sends.append((lambda src=src: src, None))
         waits.extend(swap)
 
     def scales():
@@ -645,7 +667,12 @@
 
     def give(k, part, z, p, buf, sem, peer, present=None):
         src = red[k].piece(held, k, part, z, p)
-        send(src, red[k].piece(buf, k, part, z, p), sem, peer, present)
+        group = None
+        if peer is at.second:
+            group = (("sums", k, part, 2), 2 * depth if part == 0 else 2)
+        elif peer is at.first:
+            group = (("sums", k, part, 1), depth if part == 0 else 1)
+        send(src, red[k].piece(buf, k, part, z, p), sem, peer, present, group)
 
     def take(k, part, z, p, buf, sem):
         got(red[k].piece(buf, k, part, z, p), sem)
@@ -796,15 +823,19 @@
         steps[step[0]](*step[1:])
     for j in range(per):
         out[0, j] = flat[j].T
-    for n, (like, present) in enumerate(sends):
-
-        def sent(n=n, like=like):
-            remote(like(), like(), send_sems.at[n], load_sems.at[0], at.sibling).wait_send()
+    for shared, n, kind, rows, present in sends:
+
+        def sent(shared=shared, n=n, kind=kind, rows=rows):
+            piece = like(kind, rows)
+            sem = group_sems.at[n] if shared else send_sems.at[n]
+            remote(piece, piece, sem, load_sems.at[0], at.sibling).wait_send()
 
         if present is None:
             sent()
         else:
             pl.when(present())(sent)
+    for copy in waits:
+        copy.wait_send()
 
 
 def one_section(tokens, blocks_in, blocks_out, pos_in, pos_out, cotangent):
@@ -814,7 +845,8 @@
     depth = devices // 8
     chips = devices // 2
     entries = 4 * per * chips
-    sends = 8 * depth + SLICES * (15 + 14 * depth)
+    sends = 1 + 2 * depth + SLICES * 8 * depth
+    shared = 8 * SLICES + 2
     size = BLOCK // 2 // SLICES
     ranks = RANK // BLOCK * size
     blocks = (width // BLOCK) * (RANK // BLOCK)
@@ -855,8 +887,9 @@
             vmem((SLICES, 4 * per, size, BLOCK), bf16),
             vmem((SLICES, 4 * per, size, BLOCK), bf16),
             vmem((per, BLOCK, BLOCK), bf16),
-            dma((7 + SLICES,)),
+            dma((9 + SLICES,)),
             dma((sends,)),
+            dma((shared,)),
             dma((SLICES, 2)),
             dma((SLICES, 2)),
             dma((chips + 1,)),

time: 96.3 us -> 94.6 us (0.982)
  Pallas kernels: 93.7 us -> 92.1 us
    pallas_call x1, Pallas kernels: 93.7 us -> 92.1 us  [one_section(): pl.pallas_call(functools.partial(fused_kernel, devices), out_shape=jax.Sh...]
where the time goes in v4:
time: 94.6 us; the launch traced here: 94.4 us
  Pallas kernels  92.1 us (97%)
  local copies, waits for them, and re-layouts  1.74 us (2%)
    pallas_call x1, Pallas kernels, one_section(): pl.pallas_call(functools.partial(fused_kernel, devices), out_shape=jax.Sh...  92.1 us

profile of v4, /device:TPU:1, one launch (start us, length us, event | category | flops | bytes accessed | tf_op | source)
XLA Modules:
  0.0 94.4 jit_solution(17559095786248846945)
XLA Ops:
  0.6 92.1 %fused_adapters.1 = bf16[2,5,128,128]{3,2,1,0:T(8,128)(2,1)} custom-call(s32[1,5]{1,0:T(1,128)} %pos_in.1, s32[1,5]{1,0:T(1,128)} %pos_out.1, bf16[5,128,128]{2,1,0:T(8,128)(2,1)} %bitcast.2, bf16[5,128,128]{2,1,0:T(8,128)(2,1)} %bitcast.3, bf16[128,8192]{1,0:T(8,128)(2,1)} %tokens.1, bf16[128,8192]{1,0:T(8,128)(2,1)} %cotangent.1), custom_call_target="tpu_custom_call" | custom-call | tf_op jit(solution)/shard_map/fused_adapters/pallas_call | solution.py:862
  92.7 1.7 %fusion = (bf16[1,5,128,128]{3,2,1,0:T(8,128)(2,1)}, bf16[1,5,128,128]{3,2,1,0:T(8,128)(2,1)}) fusion(bf16[2,5,128,128]{3,2,1,0:T(8,128)(2,1)} %fused_adapters.1), kind=kLoop, calls=%fused_computation | loop fusion | bytes 655360 | tf_op jit(solution)/shard_map/slice | solution.py:908

commit v5 on v4

--- a/solution.py
+++ b/solution.py
@@ -172,7 +172,7 @@
 SLICES = 2
 GATHER_PLANE = (1, 1)
 REDUCE_PLANE = (1, 1)
-CHUNK = 1024
+CHUNK = 2048
 
 def plain_order(depth):
     steps = []

time: 94.6 us -> 93.9 us (level)
  no operation moved by 1% of the time
where the time goes in v5:
time: 93.9 us; the launch traced here: 93.8 us
  Pallas kernels  91.4 us (97%)
  local copies, waits for them, and re-layouts  1.74 us (2%)
    pallas_call x1, Pallas kernels, one_section(): pl.pallas_call(functools.partial(fused_kernel, devices), out_shape=jax.Sh...  91.4 us

profile of v5, /device:TPU:1, one launch (start us, length us, event | category | flops | bytes accessed | tf_op | source)
XLA Modules:
  0.0 93.8 jit_solution(17008050203415584068)
XLA Ops:
  0.6 91.4 %fused_adapters.1 = bf16[2,5,128,128]{3,2,1,0:T(8,128)(2,1)} custom-call(s32[1,5]{1,0:T(1,128)} %pos_in.1, s32[1,5]{1,0:T(1,128)} %pos_out.1, bf16[5,128,128]{2,1,0:T(8,128)(2,1)} %bitcast.2, bf16[5,128,128]{2,1,0:T(8,128)(2,1)} %bitcast.3, bf16[128,8192]{1,0:T(8,128)(2,1)} %tokens.1, bf16[128,8192]{1,0:T(8,128)(2,1)} %cotangent.1), custom_call_target="tpu_custom_call" | custom-call | tf_op jit(solution)/shard_map/fused_adapters/pallas_call | solution.py:862
  92.0 1.7 %fusion = (bf16[1,5,128,128]{3,2,1,0:T(8,128)(2,1)}, bf16[1,5,128,128]{3,2,1,0:T(8,128)(2,1)}) fusion(bf16[2,5,128,128]{3,2,1,0:T(8,128)(2,1)} %fused_adapters.1), kind=kLoop, calls=%fused_computation | loop fusion | bytes 655360 | tf_op jit(solution)/shard_map/slice | solution.py:908
